TPU v7x, 32 devices: a whole 2x2x4 slice. The times are simulated.
32 devices in a mesh: lat: 8 (over z, core), lon: 4 (over y, x).
Axes of the slice: x: 2, y: 2, z: 4, core: 2. Of those that a mesh axis runs over, the one named last changes fastest.
Arguments:
- misfit: float32 [8, 256, 512], P(None, 'lat', 'lon'), may hold values from -6 to 6
- flow_east: float32 [8, 256, 512], P(None, 'lat', 'lon'), may hold values from -6 to 6
- flow_north: float32 [8, 256, 512], P(None, 'lat', 'lon'), may hold values from -6 to 6
- ocean_depth: float32 [256, 512], P('lat', 'lon'), may hold values from 0.4 to 1.6
- drag_rate: float32 [256, 512], P('lat', 'lon'), may hold values from 0.02 to 0.3
- wet_mask: int32 [256, 512], P('lat', 'lon'), may hold values from 0 to 1, as said below
- legendre: bfloat16 [256, 256, 1024], P(('lon', 'lat')), as said below
- love_factor: float32 [256], replicated, may hold values from 0.2 to 2
- assignment: int32 [256], replicated, may hold values from 0 to 255, as said below
Outputs:
- adjoint_height: float32 [8, 256, 512], P(None, 'lat', 'lon')
- adjoint_east: float32 [8, 256, 512], P(None, 'lat', 'lon')
- adjoint_north: float32 [8, 256, 512], P(None, 'lat', 'lon')
Inputs may be any that keep to these rules, and one draw needn't show every extreme that they name: `wet_mask`: 1 marks a wet cell and 0 land; the first and the last latitude rows are land. `assignment`: A permutation: each of the 256 orders appears once. `legendre`: entry [p, a, n] belongs to degree assignment[p] + n and is zero where assignment[p] + n >= 256.
All inputs are finite; a program needn't handle non-finite values.
Results may differ from a plain program's by a relative error of at most 0.0028.
Values may be sent and summed in bfloat16 or wider, within the bound.
A program may use at most 64 MiB of HBM per device.

v0:
```python
import math
import jax
import jax.numpy as jnp
from jax import lax
from jax.sharding import PartitionSpec as P

TIME_STEPS = 4
TWO_PI = 2.0 * math.pi
exact_mode = lax.Precision.HIGHEST


def with_halo(cells, sides, width):
    for axis, dim in sides:
        count = lax.axis_size(axis)
        head = lax.slice_in_dim(cells, 0, width, axis=dim)
        tail = lax.slice_in_dim(cells, cells.shape[dim] - width, cells.shape[dim], axis=dim)
        cells = jnp.concatenate(
            [
                lax.ppermute(tail, axis, [(i, (i + 1) % count) for i in range(count)]),
                cells,
                lax.ppermute(head, axis, [((i + 1) % count, i) for i in range(count)]),
            ],
            axis=dim,
        )
    return cells


def extend(stacked):
    return with_halo(stacked, (("lat", 2), ("lon", 3)), 1)


def differences(extended):
    east_diff = extended[:, :, 1:-1, 2:] - extended[:, :, 1:-1, :-2]
    north_diff = extended[:, :, 2:, 1:-1] - extended[:, :, :-2, 1:-1]
    return (east_diff, north_diff)


def adjoint_step(height, east_flow, north_flow, wetness, ocean_depth, drag_rate):
    east_diff, north_diff = differences(extend(height[None]))
    retained = 1.0 - drag_rate
    east_flow = wetness * (retained * east_flow - 0.5 * east_diff[0])
    north_flow = wetness * (retained * north_flow - 0.5 * north_diff[0])
    flow_east_diff, flow_north_diff = differences(extend(jnp.stack([east_flow, north_flow])))
    height = wetness * (height - 0.5 * ocean_depth * (flow_east_diff[0] + flow_north_diff[1]))
    return (height, east_flow, north_flow)


def phases(orders, positions, period):
    products = orders[:, None] * positions[None, :] % period
    radians = products.astype(jnp.float32) * (TWO_PI / period)
    return (jnp.cos(radians), jnp.sin(radians))


def spherical(spectra, legendre, weights, lat_count, row_count):
    slot_count = legendre.shape[0]
    degree_count = legendre.shape[2]
    legendre_blocks = legendre.reshape(slot_count, lat_count, row_count, degree_count)
    spectra_blocks = spectra.reshape(slot_count, lat_count, -1, row_count)
    coefficients = jnp.einsum(
        "kicr,kirn->kcn", spectra_blocks, legendre_blocks, preferred_element_type=jnp.float32
    )
    coefficients = (coefficients * weights[:, None, :]).astype(jnp.bfloat16)
    synthesis = jnp.einsum(
        "kcn,kirn->kicr", coefficients, legendre_blocks, preferred_element_type=jnp.float32
    )
    return synthesis.astype(jnp.bfloat16)


def local(
    misfit,
    flow_east,
    flow_north,
    ocean_depth,
    drag_rate,
    wet_mask,
    legendre,
    love_factor,
    assignment,
):
    field_count, row_count, col_count = misfit.shape
    lat_count = lax.axis_size("lat")
    lon_count = lax.axis_size("lon")
    period = col_count * lon_count
    order_count = period // 2
    slot_count = legendre.shape[0]
    degree_count = legendre.shape[2]
    row_pair = row_count // lon_count
    lat_index = lax.axis_index("lat")
    lon_index = lax.axis_index("lon")
    wetness = wet_mask.astype(jnp.float32)
    height = wetness * misfit
    east_flow = wetness * flow_east
    north_flow = wetness * flow_north

    def advance(height, east_flow, north_flow):
        return adjoint_step(height, east_flow, north_flow, wetness, ocean_depth, drag_rate)

    for _ in range(TIME_STEPS):
        height, east_flow, north_flow = advance(height, east_flow, north_flow)
    base = (lon_index * lat_count + lat_index) * slot_count
    my_orders = lax.dynamic_slice_in_dim(assignment, base, slot_count)
    love_pad = jnp.concatenate([love_factor, jnp.zeros((degree_count,), jnp.float32)])
    weights = jax.vmap(
        lambda first_order: lax.dynamic_slice_in_dim(love_pad, first_order, degree_count)
    )(my_orders)
    all_cells = jnp.arange(period, dtype=jnp.int32)
    cos_full, sin_full = phases(assignment, all_cells, period)
    row_block = lax.all_to_all(height, "lon", split_axis=1, concat_axis=2, tiled=True)
    real_part = jnp.einsum("nrx,mx->nrm", row_block, cos_full, precision=exact_mode)
    imag_part = -jnp.einsum("nrx,mx->nrm", row_block, sin_full, precision=exact_mode)
    rowwise = jnp.stack([real_part, imag_part], 2).astype(jnp.bfloat16)
    gathered = rowwise.transpose(3, 2, 0, 1).reshape(lon_count, lat_count, -1)
    received = lax.all_to_all(
        lax.all_to_all(gathered, "lat", split_axis=1, concat_axis=1, tiled=True),
        "lon",
        split_axis=0,
        concat_axis=0,
        tiled=True,
    )
    received = received.reshape(lon_count, lat_count, slot_count, 2, field_count, row_pair)
    spectra = received.transpose(2, 1, 3, 4, 0, 5).reshape(
        slot_count, lat_count, 2 * field_count * row_count
    )
    synthesis = spherical(spectra, legendre, weights, lat_count, row_count)
    arranged = synthesis.reshape(slot_count, lat_count, 2, field_count, lon_count, row_pair)
    arranged = arranged.transpose(4, 1, 0, 2, 3, 5).reshape(lon_count, lat_count, -1)
    returned = lax.all_to_all(
        lax.all_to_all(arranged, "lat", split_axis=1, concat_axis=1, tiled=True),
        "lon",
        split_axis=0,
        concat_axis=0,
        tiled=True,
    )
    returned = returned.reshape(order_count, 2, field_count, row_pair).astype(jnp.float32)
    doubling = jnp.where(assignment == 0, 1.0, 2.0).astype(jnp.float32)
    grid_rows = jnp.einsum(
        "mx,mfr->frx", cos_full * doubling[:, None], returned[:, 0], precision=exact_mode
    ) - jnp.einsum(
        "mx,mfr->frx", sin_full * doubling[:, None], returned[:, 1], precision=exact_mode
    )
    loading = lax.all_to_all(grid_rows, "lon", split_axis=2, concat_axis=1, tiled=True)
    height = height + wetness * loading
    return advance(height, east_flow, north_flow)


def solution(mesh):
    placed = (
        P(None, "lat", "lon"),
        P(None, "lat", "lon"),
        P(None, "lat", "lon"),
        P("lat", "lon"),
        P("lat", "lon"),
        P("lat", "lon"),
        P(("lon", "lat"), None, None),
        P(),
        P(),
    )
    return jax.shard_map(
        local,
        mesh=mesh,
        in_specs=placed,
        out_specs=(P(None, "lat", "lon"), P(None, "lat", "lon"), P(None, "lat", "lon")),
        check_vma=False,
    )
```

profile of v0, /device:TPU:0, one launch (start us, length us, event | category | flops | bytes accessed | tf_op | source)
XLA Modules:
  0.0 253.9 jit_solution(16418631101517796318)
XLA Ops:
  2.9 4.1 %collective-permute-start.1 = (f32[1,8,1,128]{3,1,2,0:T(8,128)S(1)}, f32[1,8,1,128]{3,1,2,0:T(8,128)S(1)}, u32[]{:S(2)}, u32[]{:S(2)}) collective-permute-start(f32[1,8,1,128]{3,1,2,0:T(8,128)S(1)} %get-tuple-element.71), channel_id=1, source_target_pairs={{4,0},{8,4},{12,8},{16,12},{20,16},{24,20},{28,24},{0,28},{5,1},{9... | collective-permute-start | bytes 12296 | tf_op jit(solution)/shard_map/ppermute | solution.py:21
  8.5 2.9 %collective-permute-start.2 = (f32[1,8,34,1]{3,1,2,0:T(8,128)S(1)}, f32[1,8,34,1]{3,1,2,0:T(8,128)S(1)}, u32[]{:S(2)}, u32[]{:S(2)}) collective-permute-start(f32[1,8,34,1]{3,1,2,0:T(8,128)S(1)} %get-tuple-element.61), channel_id=1, source_target_pairs={{1,0},{2,1},{3,2},{0,3},{5,4},{6,5},{7,6},{4,7},{9,8},{10,9},{11,1... | collective-permute-start | bytes 3272 | tf_op jit(solution)/shard_map/ppermute | solution.py:21
  12.1 3.3 %collective-permute-done.2 = f32[1,8,34,1]{3,1,2,0:T(8,128)S(1)} collective-permute-done((f32[1,8,34,1]{3,1,2,0:T(8,128)S(1)}, f32[1,8,34,1]{3,1,2,0:T(8,128)S(1)}, u32[]{:S(2)}, u32[]{:S(2)}) %collective-permute-start.2) | collective-permute-done | bytes 1120 | tf_op jit(solution)/shard_map/ppermute | solution.py:21
  15.5 3.1 %collective-permute-done.3 = f32[1,8,34,1]{3,1,2,0:T(8,128)S(1)} collective-permute-done((f32[1,8,34,1]{3,1,2,0:T(8,128)S(1)}, f32[1,8,34,1]{3,1,2,0:T(8,128)S(1)}, u32[]{:S(2)}, u32[]{:S(2)}) %collective-permute-start.3) | collective-permute-done | bytes 1120 | tf_op jit(solution)/shard_map/ppermute | solution.py:19
  19.8 3.5 %collective-permute-start.5 = (f32[2,8,1,128]{3,1,2,0:T(8,128)S(1)}, f32[2,8,1,128]{3,1,2,0:T(8,128)S(1)}, u32[]{:S(2)}, u32[]{:S(2)}) collective-permute-start(f32[2,8,1,128]{3,1,2,0:T(8,128)S(1)} %get-tuple-element.46), channel_id=1, source_target_pairs={{4,0},{8,4},{12,8},{16,12},{20,16},{24,20},{28,24},{0,28},{5,1},{9... | collective-permute-start | bytes 24584 | tf_op jit(solution)/shard_map/ppermute | solution.py:21
  27.7 6.8 %collective-permute-done.6 = f32[2,8,34,1]{3,1,2,0:T(8,128)S(1)} collective-permute-done((f32[2,8,34,1]{3,1,2,0:T(8,128)S(1)}, f32[2,8,34,1]{3,1,2,0:T(8,128)S(1)}, u32[]{:S(2)}, u32[]{:S(2)}) %collective-permute-start.6) | collective-permute-done | bytes 2208 | tf_op jit(solution)/shard_map/ppermute | solution.py:21
  34.5 3.3 %collective-permute-done.7 = f32[2,8,34,1]{3,1,2,0:T(8,128)S(1)} collective-permute-done((f32[2,8,34,1]{3,1,2,0:T(8,128)S(1)}, f32[2,8,34,1]{3,1,2,0:T(8,128)S(1)}, u32[]{:S(2)}, u32[]{:S(2)}) %collective-permute-start.7) | collective-permute-done | bytes 2208 | tf_op jit(solution)/shard_map/ppermute | solution.py:19
  38.0 3.5 %collective-permute-start.9 = (f32[1,8,1,128]{3,1,2,0:T(8,128)S(1)}, f32[1,8,1,128]{3,1,2,0:T(8,128)S(1)}, u32[]{:S(2)}, u32[]{:S(2)}) collective-permute-start(f32[1,8,1,128]{3,1,2,0:T(8,128)S(1)} %get-tuple-element.69), channel_id=1, source_target_pairs={{4,0},{8,4},{12,8},{16,12},{20,16},{24,20},{28,24},{0,28},{5,1},{9... | collective-permute-start | bytes 12296 | tf_op jit(solution)/shard_map/ppermute | solution.py:21
  43.0 2.4 collective-permute-start.10
  45.4 3.7 %collective-permute-done.10 = f32[1,8,34,1]{3,1,2,0:T(8,128)S(1)} collective-permute-done((f32[1,8,34,1]{3,1,2,0:T(8,128)S(1)}, f32[1,8,34,1]{3,1,2,0:T(8,128)S(1)}, u32[]{:S(2)}, u32[]{:S(2)}) %collective-permute-start.10) | collective-permute-done | bytes 1120 | tf_op jit(solution)/shard_map/ppermute | solution.py:21
  49.1 2.4 collective-permute-done.11
  51.8 3.5 %collective-permute-start.13 = (f32[2,8,1,128]{3,1,2,0:T(8,128)S(1)}, f32[2,8,1,128]{3,1,2,0:T(8,128)S(1)}, u32[]{:S(2)}, u32[]{:S(2)}) collective-permute-start(f32[2,8,1,128]{3,1,2,0:T(8,128)S(1)} %get-tuple-element.44), channel_id=1, source_target_pairs={{4,0},{8,4},{12,8},{16,12},{20,16},{24,20},{28,24},{0,28},{5,1},{9... | collective-permute-start | bytes 24584 | tf_op jit(solution)/shard_map/ppermute | solution.py:21
  59.0 7.5 %collective-permute-done.14 = f32[2,8,34,1]{3,1,2,0:T(8,128)S(1)} collective-permute-done((f32[2,8,34,1]{3,1,2,0:T(8,128)S(1)}, f32[2,8,34,1]{3,1,2,0:T(8,128)S(1)}, u32[]{:S(2)}, u32[]{:S(2)}) %collective-permute-start.14) | collective-permute-done | bytes 2208 | tf_op jit(solution)/shard_map/ppermute | solution.py:21
  66.5 2.9 %collective-permute-done.15 = f32[2,8,34,1]{3,1,2,0:T(8,128)S(1)} collective-permute-done((f32[2,8,34,1]{3,1,2,0:T(8,128)S(1)}, f32[2,8,34,1]{3,1,2,0:T(8,128)S(1)}, u32[]{:S(2)}, u32[]{:S(2)}) %collective-permute-start.15) | collective-permute-done | bytes 2208 | tf_op jit(solution)/shard_map/ppermute | solution.py:19
  69.6 3.5 %collective-permute-start.17 = (f32[1,8,1,128]{3,1,2,0:T(8,128)S(1)}, f32[1,8,1,128]{3,1,2,0:T(8,128)S(1)}, u32[]{:S(2)}, u32[]{:S(2)}) collective-permute-start(f32[1,8,1,128]{3,1,2,0:T(8,128)S(1)} %get-tuple-element.67), channel_id=1, source_target_pairs={{4,0},{8,4},{12,8},{16,12},{20,16},{24,20},{28,24},{0,28},{5,1},{9... | collective-permute-start | bytes 12296 | tf_op jit(solution)/shard_map/ppermute | solution.py:21
  74.6 2.0 collective-permute-start.18
  76.7 3.2 %collective-permute-done.18 = f32[1,8,34,1]{3,1,2,0:T(8,128)S(1)} collective-permute-done((f32[1,8,34,1]{3,1,2,0:T(8,128)S(1)}, f32[1,8,34,1]{3,1,2,0:T(8,128)S(1)}, u32[]{:S(2)}, u32[]{:S(2)}) %collective-permute-start.18) | collective-permute-done | bytes 1120 | tf_op jit(solution)/shard_map/ppermute | solution.py:21
  80.0 2.6 %collective-permute-done.19 = f32[1,8,34,1]{3,1,2,0:T(8,128)S(1)} collective-permute-done((f32[1,8,34,1]{3,1,2,0:T(8,128)S(1)}, f32[1,8,34,1]{3,1,2,0:T(8,128)S(1)}, u32[]{:S(2)}, u32[]{:S(2)}) %collective-permute-start.19) | collective-permute-done | bytes 1120 | tf_op jit(solution)/shard_map/ppermute | solution.py:19
  82.8 3.5 %collective-permute-start.21 = (f32[2,8,1,128]{3,1,2,0:T(8,128)S(1)}, f32[2,8,1,128]{3,1,2,0:T(8,128)S(1)}, u32[]{:S(2)}, u32[]{:S(2)}) collective-permute-start(f32[2,8,1,128]{3,1,2,0:T(8,128)S(1)} %get-tuple-element.42), channel_id=1, source_target_pairs={{4,0},{8,4},{12,8},{16,12},{20,16},{24,20},{28,24},{0,28},{5,1},{9... | collective-permute-start | bytes 24584 | tf_op jit(solution)/shard_map/ppermute | solution.py:21
  89.9 7.4 %collective-permute-done.22 = f32[2,8,34,1]{3,1,2,0:T(8,128)S(1)} collective-permute-done((f32[2,8,34,1]{3,1,2,0:T(8,128)S(1)}, f32[2,8,34,1]{3,1,2,0:T(8,128)S(1)}, u32[]{:S(2)}, u32[]{:S(2)}) %collective-permute-start.22) | collective-permute-done | bytes 2208 | tf_op jit(solution)/shard_map/ppermute | solution.py:21
  97.3 2.9 %collective-permute-done.23 = f32[2,8,34,1]{3,1,2,0:T(8,128)S(1)} collective-permute-done((f32[2,8,34,1]{3,1,2,0:T(8,128)S(1)}, f32[2,8,34,1]{3,1,2,0:T(8,128)S(1)}, u32[]{:S(2)}, u32[]{:S(2)}) %collective-permute-start.23) | collective-permute-done | bytes 2208 | tf_op jit(solution)/shard_map/ppermute | solution.py:19
  100.5 3.5 %collective-permute-start.25 = (f32[1,8,1,128]{3,1,2,0:T(8,128)S(1)}, f32[1,8,1,128]{3,1,2,0:T(8,128)S(1)}, u32[]{:S(2)}, u32[]{:S(2)}) collective-permute-start(f32[1,8,1,128]{3,1,2,0:T(8,128)S(1)} %get-tuple-element.65), channel_id=1, source_target_pairs={{4,0},{8,4},{12,8},{16,12},{20,16},{24,20},{28,24},{0,28},{5,1},{9... | collective-permute-start | bytes 12296 | tf_op jit(solution)/shard_map/ppermute | solution.py:21
  107.5 3.0 %collective-permute-done.26 = f32[1,8,34,1]{3,1,2,0:T(8,128)S(1)} collective-permute-done((f32[1,8,34,1]{3,1,2,0:T(8,128)S(1)}, f32[1,8,34,1]{3,1,2,0:T(8,128)S(1)}, u32[]{:S(2)}, u32[]{:S(2)}) %collective-permute-start.26) | collective-permute-done | bytes 1120 | tf_op jit(solution)/shard_map/ppermute | solution.py:21
  110.6 2.4 collective-permute-done.27
  113.3 3.5 %collective-permute-start.29 = (f32[2,8,1,128]{3,1,2,0:T(8,128)S(1)}, f32[2,8,1,128]{3,1,2,0:T(8,128)S(1)}, u32[]{:S(2)}, u32[]{:S(2)}) collective-permute-start(f32[2,8,1,128]{3,1,2,0:T(8,128)S(1)} %get-tuple-element.40), channel_id=1, source_target_pairs={{4,0},{8,4},{12,8},{16,12},{20,16},{24,20},{28,24},{0,28},{5,1},{9... | collective-permute-start | bytes 24584 | tf_op jit(solution)/shard_map/ppermute | solution.py:21
  120.4 7.5 %collective-permute-done.30 = f32[2,8,34,1]{3,1,2,0:T(8,128)S(1)} collective-permute-done((f32[2,8,34,1]{3,1,2,0:T(8,128)S(1)}, f32[2,8,34,1]{3,1,2,0:T(8,128)S(1)}, u32[]{:S(2)}, u32[]{:S(2)}) %collective-permute-start.30) | collective-permute-done | bytes 2208 | tf_op jit(solution)/shard_map/ppermute | solution.py:21
  127.9 3.2 %collective-permute-done.31 = f32[2,8,34,1]{3,1,2,0:T(8,128)S(1)} collective-permute-done((f32[2,8,34,1]{3,1,2,0:T(8,128)S(1)}, f32[2,8,34,1]{3,1,2,0:T(8,128)S(1)}, u32[]{:S(2)}, u32[]{:S(2)}) %collective-permute-start.31) | collective-permute-done | bytes 2208 | tf_op jit(solution)/shard_map/ppermute | solution.py:19
  131.3 7.7 %all_to_all.56 = f32[8,32,128]{2,0,1:T(8,128)S(1)} all-to-all(f32[8,32,128]{2,0,1:T(8,128)S(1)} %fusion.51), channel_id=1, replica_groups=mesh['lat'=8,'lon'=4] {'lon'}, dimensions={1} | all-to-all | bytes 262144 | tf_op jit(solution)/shard_map/all_to_all | solution.py:108
  139.1 2.5 fusion.5
  141.6 2.5 %fusion.6 = bf16[8,8,1,256]{3,1,0,2:T(8,128)(2,1)S(1)} fusion(s32[256]{0:T(256)S(1)} %copy-done.2, f32[8,4,8,128]{3,0,2,1:T(8,128)S(1)} %bitcast.257), kind=kOutput, calls=%fused_computation.12 | convolution fusion | flops 102531072 | bytes 164864 | tf_op jit(solution)/shard_map/nrx,mx->nrm/dot_general | solution.py:110
  147.2 3.4 %all-to-all-start.1 = ((bf16[4,8,1024]{2,0,1:T(4,128)(2,1)}), bf16[4,8,1024]{2,0,1:T(4,128)(2,1)S(1)}, u32[]{:S(2)}, u32[]{:S(2)}) async-start(bf16[4,8,1024]{2,0,1:T(4,128)(2,1)} %copy.39), calls=%async_computation.1 | async-start | bytes 131072 | tf_op jit(solution)/shard_map/all_to_all | solution.py:114
  150.6 5.8 %all-to-all-done.1 = bf16[4,8,1024]{2,0,1:T(4,128)(2,1)S(1)} async-done(((bf16[4,8,1024]{2,0,1:T(4,128)(2,1)}), bf16[4,8,1024]{2,0,1:T(4,128)(2,1)S(1)}, u32[]{:S(2)}, u32[]{:S(2)}) %all-to-all-start.1) | async-done | bytes 65568 | tf_op jit(solution)/shard_map/all_to_all | solution.py:114
  157.1 3.5 %all-to-all-start.2 = ((bf16[4,8,1024]{2,1,0:T(8,128)(2,1)}), bf16[4,8,1024]{2,1,0:T(8,128)(2,1)S(1)}, u32[]{:S(2)}, u32[]{:S(2)}) async-start(bf16[4,8,1024]{2,1,0:T(8,128)(2,1)} %copy.40), calls=%async_computation.2 | async-start | bytes 131072 | tf_op jit(solution)/shard_map/all_to_all | solution.py:113
  160.7 11.2 %while.1 = (s32[]{:T(128)}, f32[1280]{0:T(1024)S(1)}, s32[8,1]{0,1:T(1,128)S(1)}, f32[8,1024]{1,0:T(8,128)S(1)}, s32[]{:T(128)}, /*index=5*/s32[]{:T(128)}) while((s32[]{:T(128)}, f32[1280]{0:T(1024)S(1)}, s32[8,1]{0,1:T(1,128)S(1)}, f32[8,1024]{1,0:T(8,128)S(1)}, s32[]{:T(128)}, /*index=5*/s32[]{:T(128)}) %tuple.46), condition=%wide.while_cond, body=%wide.while_body.sunk | while | flops 2 | bytes 16473 | solution.py:104
  175.0 7.1 %fusion.3 = bf16[8,8,16,32]{3,2,1,0:T(8,128)(2,1)S(1)} fusion(bf16[8,8,32,1024]{3,2,1,0:T(8,128)(2,1)} %bitcast.210, bf16[8,8,16,32]{3,2,1,0:T(8,128)(2,1)S(1)} %reshape_reshape.3, f32[8,1024]{1,0:T(8,128)S(1)} %get-tuple-element.10), kind=kOutput, calls=%fused_computation.6 | convolution fusion | flops 134512640 | bytes 4358144 | tf_op jit(solution)/shard_map/kcn,kirn->kicr/dot_general | solution.py:63
  184.2 8.3 %all_to_all.57 = bf16[4,8,1024]{2,0,1:T(4,128)(2,1)S(1)} all-to-all(bf16[4,8,1024]{2,0,1:T(4,128)(2,1)S(1)} %copy.43), channel_id=1, replica_groups=mesh['lat'=8,'lon'=4] {'lat'}, dimensions={1} | all-to-all | bytes 131072 | tf_op jit(solution)/shard_map/all_to_all | solution.py:128
  193.2 3.9 %all-to-all-start.4 = ((bf16[4,8,1024]{2,1,0:T(8,128)(2,1)}), bf16[4,8,1024]{2,1,0:T(8,128)(2,1)S(1)}, u32[]{:S(2)}, u32[]{:S(2)}) async-start(bf16[4,8,1024]{2,1,0:T(8,128)(2,1)} %copy.44), calls=%async_computation.4 | async-start | bytes 131072 | tf_op jit(solution)/shard_map/all_to_all | solution.py:127
  197.1 4.8 %all-to-all-done.4 = bf16[4,8,1024]{2,1,0:T(8,128)(2,1)S(1)} async-done(((bf16[4,8,1024]{2,1,0:T(8,128)(2,1)}), bf16[4,8,1024]{2,1,0:T(8,128)(2,1)S(1)}, u32[]{:S(2)}, u32[]{:S(2)}) %all-to-all-start.4) | async-done | bytes 65568 | tf_op jit(solution)/shard_map/all_to_all | solution.py:127
  203.9 2.3 fusion.11
  206.2 2.3 convolution_subtract_fusion
  210.3 7.4 %all_to_all.58 = f32[4,1,8192]{2,1,0:T(1,128)S(1)} all-to-all(f32[4,1,8192]{2,1,0:T(1,128)S(1)} %reshape.81), channel_id=1, replica_groups=mesh['lat'=8,'lon'=4] {'lon'}, dimensions={0} | all-to-all | bytes 262144 | tf_op jit(solution)/shard_map/all_to_all | solution.py:141
  221.1 3.5 %collective-permute-start.33 = (f32[1,8,1,128]{3,1,2,0:T(8,128)S(1)}, f32[1,8,1,128]{3,1,2,0:T(8,128)S(1)}, u32[]{:S(2)}, u32[]{:S(2)}) collective-permute-start(f32[1,8,1,128]{3,1,2,0:T(8,128)S(1)} %get-tuple-element.63), channel_id=1, source_target_pairs={{4,0},{8,4},{12,8},{16,12},{20,16},{24,20},{28,24},{0,28},{5,1},{9... | collective-permute-start | bytes 12296 | tf_op jit(solution)/shard_map/ppermute | solution.py:21
  228.2 4.3 %collective-permute-done.34 = f32[1,8,34,1]{3,1,2,0:T(8,128)S(1)} collective-permute-done((f32[1,8,34,1]{3,1,2,0:T(8,128)S(1)}, f32[1,8,34,1]{3,1,2,0:T(8,128)S(1)}, u32[]{:S(2)}, u32[]{:S(2)}) %collective-permute-start.34) | collective-permute-done | bytes 1120 | tf_op jit(solution)/shard_map/ppermute | solution.py:21
  232.5 1.8 collective-permute-done.35
  234.6 3.5 %collective-permute-start.37 = (f32[2,8,1,128]{3,1,2,0:T(8,128)S(1)}, f32[2,8,1,128]{3,1,2,0:T(8,128)S(1)}, u32[]{:S(2)}, u32[]{:S(2)}) collective-permute-start(f32[2,8,1,128]{3,1,2,0:T(8,128)S(1)} %get-tuple-element.38), channel_id=1, source_target_pairs={{4,0},{8,4},{12,8},{16,12},{20,16},{24,20},{28,24},{0,28},{5,1},{9... | collective-permute-start | bytes 24584 | tf_op jit(solution)/shard_map/ppermute | solution.py:21
  239.6 1.5 collective-permute-start.38
  243.1 6.1 %collective-permute-done.38 = f32[2,8,34,1]{3,1,2,0:T(8,128)S(1)} collective-permute-done((f32[2,8,34,1]{3,1,2,0:T(8,128)S(1)}, f32[2,8,34,1]{3,1,2,0:T(8,128)S(1)}, u32[]{:S(2)}, u32[]{:S(2)}) %collective-permute-start.38) | collective-permute-done | bytes 2208 | tf_op jit(solution)/shard_map/ppermute | solution.py:21
  249.2 3.8 %collective-permute-done.39 = f32[2,8,34,1]{3,1,2,0:T(8,128)S(1)} collective-permute-done((f32[2,8,34,1]{3,1,2,0:T(8,128)S(1)}, f32[2,8,34,1]{3,1,2,0:T(8,128)S(1)}, u32[]{:S(2)}, u32[]{:S(2)}) %collective-permute-start.39) | collective-permute-done | bytes 2208 | tf_op jit(solution)/shard_map/ppermute | solution.py:19
  (154 shorter events, 64.8 us)
Async XLA Ops:
  0.6 37.1 %copy-start = (f32[8,32,128]{2,1,0:T(8,128)S(1)}, f32[8,32,128]{2,1,0:T(8,128)}, u32[]{:S(2)}) copy-start(f32[8,32,128]{2,1,0:T(8,128)} %param.9) | copy-start | bytes 393220
  2.4 5.9 %collective-permute-start = (f32[1,8,1,128]{3,1,2,0:T(8,128)S(1)}, f32[1,8,1,128]{3,1,2,0:T(8,128)S(1)}, u32[]{:S(2)}, u32[]{:S(2)}) collective-permute-start(f32[1,8,1,128]{3,1,2,0:T(8,128)S(1)} %get-tuple-element.72), channel_id=1, source_target_pairs={{0,4},{4,8},{8,12},{12,16},{16,20},{20,24},{24,28},{28,0},{1,5},{5... | collective-permute-start | bytes 12296 | tf_op jit(solution)/shard_map/ppermute | solution.py:19
  2.9 5.4 %collective-permute-start.1 = (f32[1,8,1,128]{3,1,2,0:T(8,128)S(1)}, f32[1,8,1,128]{3,1,2,0:T(8,128)S(1)}, u32[]{:S(2)}, u32[]{:S(2)}) collective-permute-start(f32[1,8,1,128]{3,1,2,0:T(8,128)S(1)} %get-tuple-element.71), channel_id=1, source_target_pairs={{4,0},{8,4},{12,8},{16,12},{20,16},{24,20},{28,24},{0,28},{5,1},{9... | collective-permute-start | bytes 12296 | tf_op jit(solution)/shard_map/ppermute | solution.py:21
  8.5 7.0 %collective-permute-start.2 = (f32[1,8,34,1]{3,1,2,0:T(8,128)S(1)}, f32[1,8,34,1]{3,1,2,0:T(8,128)S(1)}, u32[]{:S(2)}, u32[]{:S(2)}) collective-permute-start(f32[1,8,34,1]{3,1,2,0:T(8,128)S(1)} %get-tuple-element.61), channel_id=1, source_target_pairs={{1,0},{2,1},{3,2},{0,3},{5,4},{6,5},{7,6},{4,7},{9,8},{10,9},{11,1... | collective-permute-start | bytes 3272 | tf_op jit(solution)/shard_map/ppermute | solution.py:21
  11.4 7.1 %collective-permute-start.3 = (f32[1,8,34,1]{3,1,2,0:T(8,128)S(1)}, f32[1,8,34,1]{3,1,2,0:T(8,128)S(1)}, u32[]{:S(2)}, u32[]{:S(2)}) collective-permute-start(f32[1,8,34,1]{3,1,2,0:T(8,128)S(1)} %get-tuple-element.62), channel_id=1, source_target_pairs={{0,1},{1,2},{2,3},{3,0},{4,5},{5,6},{6,7},{7,4},{8,9},{9,10},{10,1... | collective-permute-start | bytes 3272 | tf_op jit(solution)/shard_map/ppermute | solution.py:19
  19.8 4.9 %collective-permute-start.4 = (f32[2,8,1,128]{3,1,2,0:T(8,128)S(1)}, f32[2,8,1,128]{3,1,2,0:T(8,128)S(1)}, u32[]{:S(2)}, u32[]{:S(2)}) collective-permute-start(f32[2,8,1,128]{3,1,2,0:T(8,128)S(1)} %get-tuple-element.45), channel_id=1, source_target_pairs={{0,4},{4,8},{8,12},{12,16},{16,20},{20,24},{24,28},{28,0},{1,5},{5... | collective-permute-start | bytes 24584 | tf_op jit(solution)/shard_map/ppermute | solution.py:19
  19.8 4.9 %collective-permute-start.5 = (f32[2,8,1,128]{3,1,2,0:T(8,128)S(1)}, f32[2,8,1,128]{3,1,2,0:T(8,128)S(1)}, u32[]{:S(2)}, u32[]{:S(2)}) collective-permute-start(f32[2,8,1,128]{3,1,2,0:T(8,128)S(1)} %get-tuple-element.46), channel_id=1, source_target_pairs={{4,0},{8,4},{12,8},{16,12},{20,16},{24,20},{28,24},{0,28},{5,1},{9... | collective-permute-start | bytes 24584 | tf_op jit(solution)/shard_map/ppermute | solution.py:21
  24.9 9.6 %collective-permute-start.6 = (f32[2,8,34,1]{3,1,2,0:T(8,128)S(1)}, f32[2,8,34,1]{3,1,2,0:T(8,128)S(1)}, u32[]{:S(2)}, u32[]{:S(2)}) collective-permute-start(f32[2,8,34,1]{3,1,2,0:T(8,128)S(1)} %get-tuple-element.36), channel_id=1, source_target_pairs={{1,0},{2,1},{3,2},{0,3},{5,4},{6,5},{7,6},{4,7},{9,8},{10,9},{11,1... | collective-permute-start | bytes 6536 | tf_op jit(solution)/shard_map/ppermute | solution.py:21
  26.4 11.4 %collective-permute-start.7 = (f32[2,8,34,1]{3,1,2,0:T(8,128)S(1)}, f32[2,8,34,1]{3,1,2,0:T(8,128)S(1)}, u32[]{:S(2)}, u32[]{:S(2)}) collective-permute-start(f32[2,8,34,1]{3,1,2,0:T(8,128)S(1)} %get-tuple-element.35), channel_id=1, source_target_pairs={{0,1},{1,2},{2,3},{3,0},{4,5},{5,6},{6,7},{7,4},{8,9},{9,10},{10,1... | collective-permute-start | bytes 6536 | tf_op jit(solution)/shard_map/ppermute | solution.py:19
  38.0 4.9 %collective-permute-start.8 = (f32[1,8,1,128]{3,1,2,0:T(8,128)S(1)}, f32[1,8,1,128]{3,1,2,0:T(8,128)S(1)}, u32[]{:S(2)}, u32[]{:S(2)}) collective-permute-start(f32[1,8,1,128]{3,1,2,0:T(8,128)S(1)} %get-tuple-element.70), channel_id=1, source_target_pairs={{0,4},{4,8},{8,12},{12,16},{16,20},{20,24},{24,28},{28,0},{1,5},{5... | collective-permute-start | bytes 12296 | tf_op jit(solution)/shard_map/ppermute | solution.py:19
  38.0 4.9 %collective-permute-start.9 = (f32[1,8,1,128]{3,1,2,0:T(8,128)S(1)}, f32[1,8,1,128]{3,1,2,0:T(8,128)S(1)}, u32[]{:S(2)}, u32[]{:S(2)}) collective-permute-start(f32[1,8,1,128]{3,1,2,0:T(8,128)S(1)} %get-tuple-element.69), channel_id=1, source_target_pairs={{4,0},{8,4},{12,8},{16,12},{20,16},{24,20},{28,24},{0,28},{5,1},{9... | collective-permute-start | bytes 12296 | tf_op jit(solution)/shard_map/ppermute | solution.py:21
  43.0 6.1 %collective-permute-start.10 = (f32[1,8,34,1]{3,1,2,0:T(8,128)S(1)}, f32[1,8,34,1]{3,1,2,0:T(8,128)S(1)}, u32[]{:S(2)}, u32[]{:S(2)}) collective-permute-start(f32[1,8,34,1]{3,1,2,0:T(8,128)S(1)} %get-tuple-element.59), channel_id=1, source_target_pairs={{1,0},{2,1},{3,2},{0,3},{5,4},{6,5},{7,6},{4,7},{9,8},{10,9},{11,1... | collective-permute-start | bytes 3272 | tf_op jit(solution)/shard_map/ppermute | solution.py:21
  45.4 6.2 %collective-permute-start.11 = (f32[1,8,34,1]{3,1,2,0:T(8,128)S(1)}, f32[1,8,34,1]{3,1,2,0:T(8,128)S(1)}, u32[]{:S(2)}, u32[]{:S(2)}) collective-permute-start(f32[1,8,34,1]{3,1,2,0:T(8,128)S(1)} %get-tuple-element.60), channel_id=1, source_target_pairs={{0,1},{1,2},{2,3},{3,0},{4,5},{5,6},{6,7},{7,4},{8,9},{9,10},{10,1... | collective-permute-start | bytes 3272 | tf_op jit(solution)/shard_map/ppermute | solution.py:19
  51.8 4.9 %collective-permute-start.12 = (f32[2,8,1,128]{3,1,2,0:T(8,128)S(1)}, f32[2,8,1,128]{3,1,2,0:T(8,128)S(1)}, u32[]{:S(2)}, u32[]{:S(2)}) collective-permute-start(f32[2,8,1,128]{3,1,2,0:T(8,128)S(1)} %get-tuple-element.43), channel_id=1, source_target_pairs={{0,4},{4,8},{8,12},{12,16},{16,20},{20,24},{24,28},{28,0},{1,5},{5... | collective-permute-start | bytes 24584 | tf_op jit(solution)/shard_map/ppermute | solution.py:19
  51.8 4.9 %collective-permute-start.13 = (f32[2,8,1,128]{3,1,2,0:T(8,128)S(1)}, f32[2,8,1,128]{3,1,2,0:T(8,128)S(1)}, u32[]{:S(2)}, u32[]{:S(2)}) collective-permute-start(f32[2,8,1,128]{3,1,2,0:T(8,128)S(1)} %get-tuple-element.44), channel_id=1, source_target_pairs={{4,0},{8,4},{12,8},{16,12},{20,16},{24,20},{28,24},{0,28},{5,1},{9... | collective-permute-start | bytes 24584 | tf_op jit(solution)/shard_map/ppermute | solution.py:21
  56.9 9.6 %collective-permute-start.14 = (f32[2,8,34,1]{3,1,2,0:T(8,128)S(1)}, f32[2,8,34,1]{3,1,2,0:T(8,128)S(1)}, u32[]{:S(2)}, u32[]{:S(2)}) collective-permute-start(f32[2,8,34,1]{3,1,2,0:T(8,128)S(1)} %get-tuple-element.34), channel_id=1, source_target_pairs={{1,0},{2,1},{3,2},{0,3},{5,4},{6,5},{7,6},{4,7},{9,8},{10,9},{11,1... | collective-permute-start | bytes 6536 | tf_op jit(solution)/shard_map/ppermute | solution.py:21
  57.8 11.6 %collective-permute-start.15 = (f32[2,8,34,1]{3,1,2,0:T(8,128)S(1)}, f32[2,8,34,1]{3,1,2,0:T(8,128)S(1)}, u32[]{:S(2)}, u32[]{:S(2)}) collective-permute-start(f32[2,8,34,1]{3,1,2,0:T(8,128)S(1)} %get-tuple-element.33), channel_id=1, source_target_pairs={{0,1},{1,2},{2,3},{3,0},{4,5},{5,6},{6,7},{7,4},{8,9},{9,10},{10,1... | collective-permute-start | bytes 6536 | tf_op jit(solution)/shard_map/ppermute | solution.py:19
  69.6 4.9 %collective-permute-start.16 = (f32[1,8,1,128]{3,1,2,0:T(8,128)S(1)}, f32[1,8,1,128]{3,1,2,0:T(8,128)S(1)}, u32[]{:S(2)}, u32[]{:S(2)}) collective-permute-start(f32[1,8,1,128]{3,1,2,0:T(8,128)S(1)} %get-tuple-element.68), channel_id=1, source_target_pairs={{0,4},{4,8},{8,12},{12,16},{16,20},{20,24},{24,28},{28,0},{1,5},{5... | collective-permute-start | bytes 12296 | tf_op jit(solution)/shard_map/ppermute | solution.py:19
  69.6 4.9 %collective-permute-start.17 = (f32[1,8,1,128]{3,1,2,0:T(8,128)S(1)}, f32[1,8,1,128]{3,1,2,0:T(8,128)S(1)}, u32[]{:S(2)}, u32[]{:S(2)}) collective-permute-start(f32[1,8,1,128]{3,1,2,0:T(8,128)S(1)} %get-tuple-element.67), channel_id=1, source_target_pairs={{4,0},{8,4},{12,8},{16,12},{20,16},{24,20},{28,24},{0,28},{5,1},{9... | collective-permute-start | bytes 12296 | tf_op jit(solution)/shard_map/ppermute | solution.py:21
  74.6 5.3 %collective-permute-start.18 = (f32[1,8,34,1]{3,1,2,0:T(8,128)S(1)}, f32[1,8,34,1]{3,1,2,0:T(8,128)S(1)}, u32[]{:S(2)}, u32[]{:S(2)}) collective-permute-start(f32[1,8,34,1]{3,1,2,0:T(8,128)S(1)} %get-tuple-element.57), channel_id=1, source_target_pairs={{1,0},{2,1},{3,2},{0,3},{5,4},{6,5},{7,6},{4,7},{9,8},{10,9},{11,1... | collective-permute-start | bytes 3272 | tf_op jit(solution)/shard_map/ppermute | solution.py:21
  76.6 6.0 %collective-permute-start.19 = (f32[1,8,34,1]{3,1,2,0:T(8,128)S(1)}, f32[1,8,34,1]{3,1,2,0:T(8,128)S(1)}, u32[]{:S(2)}, u32[]{:S(2)}) collective-permute-start(f32[1,8,34,1]{3,1,2,0:T(8,128)S(1)} %get-tuple-element.58), channel_id=1, source_target_pairs={{0,1},{1,2},{2,3},{3,0},{4,5},{5,6},{6,7},{7,4},{8,9},{9,10},{10,1... | collective-permute-start | bytes 3272 | tf_op jit(solution)/shard_map/ppermute | solution.py:19
  82.7 56.3 %copy-start.2 = (s32[256]{0:T(256)S(1)}, s32[256]{0:T(256)}, u32[]{:S(2)}) copy-start(s32[256]{0:T(256)} %param.17) | copy-start | bytes 3076
  82.7 4.9 %collective-permute-start.20 = (f32[2,8,1,128]{3,1,2,0:T(8,128)S(1)}, f32[2,8,1,128]{3,1,2,0:T(8,128)S(1)}, u32[]{:S(2)}, u32[]{:S(2)}) collective-permute-start(f32[2,8,1,128]{3,1,2,0:T(8,128)S(1)} %get-tuple-element.41), channel_id=1, source_target_pairs={{0,4},{4,8},{8,12},{12,16},{16,20},{20,24},{24,28},{28,0},{1,5},{5... | collective-permute-start | bytes 24584 | tf_op jit(solution)/shard_map/ppermute | solution.py:19
  82.8 4.9 %collective-permute-start.21 = (f32[2,8,1,128]{3,1,2,0:T(8,128)S(1)}, f32[2,8,1,128]{3,1,2,0:T(8,128)S(1)}, u32[]{:S(2)}, u32[]{:S(2)}) collective-permute-start(f32[2,8,1,128]{3,1,2,0:T(8,128)S(1)} %get-tuple-element.42), channel_id=1, source_target_pairs={{4,0},{8,4},{12,8},{16,12},{20,16},{24,20},{28,24},{0,28},{5,1},{9... | collective-permute-start | bytes 24584 | tf_op jit(solution)/shard_map/ppermute | solution.py:21
  87.9 9.4 %collective-permute-start.22 = (f32[2,8,34,1]{3,1,2,0:T(8,128)S(1)}, f32[2,8,34,1]{3,1,2,0:T(8,128)S(1)}, u32[]{:S(2)}, u32[]{:S(2)}) collective-permute-start(f32[2,8,34,1]{3,1,2,0:T(8,128)S(1)} %get-tuple-element.32), channel_id=1, source_target_pairs={{1,0},{2,1},{3,2},{0,3},{5,4},{6,5},{7,6},{4,7},{9,8},{10,9},{11,1... | collective-permute-start | bytes 6536 | tf_op jit(solution)/shard_map/ppermute | solution.py:21
  88.4 11.8 %collective-permute-start.23 = (f32[2,8,34,1]{3,1,2,0:T(8,128)S(1)}, f32[2,8,34,1]{3,1,2,0:T(8,128)S(1)}, u32[]{:S(2)}, u32[]{:S(2)}) collective-permute-start(f32[2,8,34,1]{3,1,2,0:T(8,128)S(1)} %get-tuple-element.31), channel_id=1, source_target_pairs={{0,1},{1,2},{2,3},{3,0},{4,5},{5,6},{6,7},{7,4},{8,9},{9,10},{10,1... | collective-permute-start | bytes 6536 | tf_op jit(solution)/shard_map/ppermute | solution.py:19
  100.4 4.9 %collective-permute-start.24 = (f32[1,8,1,128]{3,1,2,0:T(8,128)S(1)}, f32[1,8,1,128]{3,1,2,0:T(8,128)S(1)}, u32[]{:S(2)}, u32[]{:S(2)}) collective-permute-start(f32[1,8,1,128]{3,1,2,0:T(8,128)S(1)} %get-tuple-element.66), channel_id=1, source_target_pairs={{0,4},{4,8},{8,12},{12,16},{16,20},{20,24},{24,28},{28,0},{1,5},{5... | collective-permute-start | bytes 12296 | tf_op jit(solution)/shard_map/ppermute | solution.py:19
  100.5 4.9 %collective-permute-start.25 = (f32[1,8,1,128]{3,1,2,0:T(8,128)S(1)}, f32[1,8,1,128]{3,1,2,0:T(8,128)S(1)}, u32[]{:S(2)}, u32[]{:S(2)}) collective-permute-start(f32[1,8,1,128]{3,1,2,0:T(8,128)S(1)} %get-tuple-element.65), channel_id=1, source_target_pairs={{4,0},{8,4},{12,8},{16,12},{20,16},{24,20},{28,24},{0,28},{5,1},{9... | collective-permute-start | bytes 12296 | tf_op jit(solution)/shard_map/ppermute | solution.py:21
  105.5 5.1 %collective-permute-start.26 = (f32[1,8,34,1]{3,1,2,0:T(8,128)S(1)}, f32[1,8,34,1]{3,1,2,0:T(8,128)S(1)}, u32[]{:S(2)}, u32[]{:S(2)}) collective-permute-start(f32[1,8,34,1]{3,1,2,0:T(8,128)S(1)} %get-tuple-element.55), channel_id=1, source_target_pairs={{1,0},{2,1},{3,2},{0,3},{5,4},{6,5},{7,6},{4,7},{9,8},{10,9},{11,1... | collective-permute-start | bytes 3272 | tf_op jit(solution)/shard_map/ppermute | solution.py:21
  106.9 6.1 %collective-permute-start.27 = (f32[1,8,34,1]{3,1,2,0:T(8,128)S(1)}, f32[1,8,34,1]{3,1,2,0:T(8,128)S(1)}, u32[]{:S(2)}, u32[]{:S(2)}) collective-permute-start(f32[1,8,34,1]{3,1,2,0:T(8,128)S(1)} %get-tuple-element.56), channel_id=1, source_target_pairs={{0,1},{1,2},{2,3},{3,0},{4,5},{5,6},{6,7},{7,4},{8,9},{9,10},{10,1... | collective-permute-start | bytes 3272 | tf_op jit(solution)/shard_map/ppermute | solution.py:19
  113.2 4.9 %collective-permute-start.28 = (f32[2,8,1,128]{3,1,2,0:T(8,128)S(1)}, f32[2,8,1,128]{3,1,2,0:T(8,128)S(1)}, u32[]{:S(2)}, u32[]{:S(2)}) collective-permute-start(f32[2,8,1,128]{3,1,2,0:T(8,128)S(1)} %get-tuple-element.39), channel_id=1, source_target_pairs={{0,4},{4,8},{8,12},{12,16},{16,20},{20,24},{24,28},{28,0},{1,5},{5... | collective-permute-start | bytes 24584 | tf_op jit(solution)/shard_map/ppermute | solution.py:19
  113.3 4.9 %collective-permute-start.29 = (f32[2,8,1,128]{3,1,2,0:T(8,128)S(1)}, f32[2,8,1,128]{3,1,2,0:T(8,128)S(1)}, u32[]{:S(2)}, u32[]{:S(2)}) collective-permute-start(f32[2,8,1,128]{3,1,2,0:T(8,128)S(1)} %get-tuple-element.40), channel_id=1, source_target_pairs={{4,0},{8,4},{12,8},{16,12},{20,16},{24,20},{28,24},{0,28},{5,1},{9... | collective-permute-start | bytes 24584 | tf_op jit(solution)/shard_map/ppermute | solution.py:21
  118.3 9.6 %collective-permute-start.30 = (f32[2,8,34,1]{3,1,2,0:T(8,128)S(1)}, f32[2,8,34,1]{3,1,2,0:T(8,128)S(1)}, u32[]{:S(2)}, u32[]{:S(2)}) collective-permute-start(f32[2,8,34,1]{3,1,2,0:T(8,128)S(1)} %get-tuple-element.30), channel_id=1, source_target_pairs={{1,0},{2,1},{3,2},{0,3},{5,4},{6,5},{7,6},{4,7},{9,8},{10,9},{11,1... | collective-permute-start | bytes 6536 | tf_op jit(solution)/shard_map/ppermute | solution.py:21
  118.9 41.8 %copy-start.1 = (f32[256]{0:T(256)S(1)}, f32[256]{0:T(256)}, u32[]{:S(2)}) copy-start(f32[256]{0:T(256)} %param.16) | copy-start | bytes 3076
  118.9 12.2 %collective-permute-start.31 = (f32[2,8,34,1]{3,1,2,0:T(8,128)S(1)}, f32[2,8,34,1]{3,1,2,0:T(8,128)S(1)}, u32[]{:S(2)}, u32[]{:S(2)}) collective-permute-start(f32[2,8,34,1]{3,1,2,0:T(8,128)S(1)} %get-tuple-element.29), channel_id=1, source_target_pairs={{0,1},{1,2},{2,3},{3,0},{4,5},{5,6},{6,7},{7,4},{8,9},{9,10},{10,1... | collective-permute-start | bytes 6536 | tf_op jit(solution)/shard_map/ppermute | solution.py:19
  147.2 9.2 %all-to-all-start.1 = ((bf16[4,8,1024]{2,0,1:T(4,128)(2,1)}), bf16[4,8,1024]{2,0,1:T(4,128)(2,1)S(1)}, u32[]{:S(2)}, u32[]{:S(2)}) async-start(bf16[4,8,1024]{2,0,1:T(4,128)(2,1)} %copy.39), calls=%async_computation.1 | async-start | bytes 131072 | tf_op jit(solution)/shard_map/all_to_all | solution.py:114
  157.1 14.8 %all-to-all-start.2 = ((bf16[4,8,1024]{2,1,0:T(8,128)(2,1)}), bf16[4,8,1024]{2,1,0:T(8,128)(2,1)S(1)}, u32[]{:S(2)}, u32[]{:S(2)}) async-start(bf16[4,8,1024]{2,1,0:T(8,128)(2,1)} %copy.40), calls=%async_computation.2 | async-start | bytes 131072 | tf_op jit(solution)/shard_map/all_to_all | solution.py:113
  193.2 8.8 %all-to-all-start.4 = ((bf16[4,8,1024]{2,1,0:T(8,128)(2,1)}), bf16[4,8,1024]{2,1,0:T(8,128)(2,1)S(1)}, u32[]{:S(2)}, u32[]{:S(2)}) async-start(bf16[4,8,1024]{2,1,0:T(8,128)(2,1)} %copy.44), calls=%async_computation.4 | async-start | bytes 131072 | tf_op jit(solution)/shard_map/all_to_all | solution.py:127
  221.0 4.9 %collective-permute-start.32 = (f32[1,8,1,128]{3,1,2,0:T(8,128)S(1)}, f32[1,8,1,128]{3,1,2,0:T(8,128)S(1)}, u32[]{:S(2)}, u32[]{:S(2)}) collective-permute-start(f32[1,8,1,128]{3,1,2,0:T(8,128)S(1)} %get-tuple-element.64), channel_id=1, source_target_pairs={{0,4},{4,8},{8,12},{12,16},{16,20},{20,24},{24,28},{28,0},{1,5},{5... | collective-permute-start | bytes 12296 | tf_op jit(solution)/shard_map/ppermute | solution.py:19
  221.1 4.9 %collective-permute-start.33 = (f32[1,8,1,128]{3,1,2,0:T(8,128)S(1)}, f32[1,8,1,128]{3,1,2,0:T(8,128)S(1)}, u32[]{:S(2)}, u32[]{:S(2)}) collective-permute-start(f32[1,8,1,128]{3,1,2,0:T(8,128)S(1)} %get-tuple-element.63), channel_id=1, source_target_pairs={{4,0},{8,4},{12,8},{16,12},{20,16},{24,20},{28,24},{0,28},{5,1},{9... | collective-permute-start | bytes 12296 | tf_op jit(solution)/shard_map/ppermute | solution.py:21
  226.0 6.5 %collective-permute-start.34 = (f32[1,8,34,1]{3,1,2,0:T(8,128)S(1)}, f32[1,8,34,1]{3,1,2,0:T(8,128)S(1)}, u32[]{:S(2)}, u32[]{:S(2)}) collective-permute-start(f32[1,8,34,1]{3,1,2,0:T(8,128)S(1)} %get-tuple-element.53), channel_id=1, source_target_pairs={{1,0},{2,1},{3,2},{0,3},{5,4},{6,5},{7,6},{4,7},{9,8},{10,9},{11,1... | collective-permute-start | bytes 3272 | tf_op jit(solution)/shard_map/ppermute | solution.py:21
  226.8 7.5 %collective-permute-start.35 = (f32[1,8,34,1]{3,1,2,0:T(8,128)S(1)}, f32[1,8,34,1]{3,1,2,0:T(8,128)S(1)}, u32[]{:S(2)}, u32[]{:S(2)}) collective-permute-start(f32[1,8,34,1]{3,1,2,0:T(8,128)S(1)} %get-tuple-element.54), channel_id=1, source_target_pairs={{0,1},{1,2},{2,3},{3,0},{4,5},{5,6},{6,7},{7,4},{8,9},{9,10},{10,1... | collective-permute-start | bytes 3272 | tf_op jit(solution)/shard_map/ppermute | solution.py:19
  234.5 4.9 %collective-permute-start.36 = (f32[2,8,1,128]{3,1,2,0:T(8,128)S(1)}, f32[2,8,1,128]{3,1,2,0:T(8,128)S(1)}, u32[]{:S(2)}, u32[]{:S(2)}) collective-permute-start(f32[2,8,1,128]{3,1,2,0:T(8,128)S(1)} %get-tuple-element.37), channel_id=1, source_target_pairs={{0,4},{4,8},{8,12},{12,16},{16,20},{20,24},{24,28},{28,0},{1,5},{5... | collective-permute-start | bytes 24584 | tf_op jit(solution)/shard_map/ppermute | solution.py:19
  234.6 4.9 %collective-permute-start.37 = (f32[2,8,1,128]{3,1,2,0:T(8,128)S(1)}, f32[2,8,1,128]{3,1,2,0:T(8,128)S(1)}, u32[]{:S(2)}, u32[]{:S(2)}) collective-permute-start(f32[2,8,1,128]{3,1,2,0:T(8,128)S(1)} %get-tuple-element.38), channel_id=1, source_target_pairs={{4,0},{8,4},{12,8},{16,12},{20,16},{24,20},{28,24},{0,28},{5,1},{9... | collective-permute-start | bytes 24584 | tf_op jit(solution)/shard_map/ppermute | solution.py:21
  239.6 9.6 %collective-permute-start.38 = (f32[2,8,34,1]{3,1,2,0:T(8,128)S(1)}, f32[2,8,34,1]{3,1,2,0:T(8,128)S(1)}, u32[]{:S(2)}, u32[]{:S(2)}) collective-permute-start(f32[2,8,34,1]{3,1,2,0:T(8,128)S(1)} %get-tuple-element.28), channel_id=1, source_target_pairs={{1,0},{2,1},{3,2},{0,3},{5,4},{6,5},{7,6},{4,7},{9,8},{10,9},{11,1... | collective-permute-start | bytes 6536 | tf_op jit(solution)/shard_map/ppermute | solution.py:21
  241.1 11.9 %collective-permute-start.39 = (f32[2,8,34,1]{3,1,2,0:T(8,128)S(1)}, f32[2,8,34,1]{3,1,2,0:T(8,128)S(1)}, u32[]{:S(2)}, u32[]{:S(2)}) collective-permute-start(f32[2,8,34,1]{3,1,2,0:T(8,128)S(1)} %get-tuple-element.27), channel_id=1, source_target_pairs={{0,1},{1,2},{2,3},{3,0},{4,5},{5,6},{6,7},{7,4},{8,9},{9,10},{10,1... | collective-permute-start | bytes 6536 | tf_op jit(solution)/shard_map/ppermute | solution.py:19
where the time goes:
time: 255 us; the launch traced here: 254 us
  waiting for transfers between devices  106 us (42%)
  starting transfers between devices  69.7 us (27%)
  local copies, waits for them, and re-layouts  29.8 us (12%)
  blocking collectives  23.4 us (9%)
  matrix products  16.7 us (7%)
  other arithmetic  7.33 us (3%)
    ppermute x20, waiting for transfers between devices, with_halo(): lax.ppermute(head, axis, [((i + 1) % count, i) for i in range(count)])  53.3 us
    ppermute x20, starting transfers between devices, with_halo(): lax.ppermute(head, axis, [((i + 1) % count, i) for i in range(count)])  50.4 us
    ppermute x20, waiting for transfers between devices, with_halo(): lax.ppermute(tail, axis, [(i, (i + 1) % count) for i in range(count)])  41.6 us
    gather x24, local copies, waits for them, and re-layouts  11 us
    ppermute x20, starting transfers between devices, with_halo(): lax.ppermute(tail, axis, [(i, (i + 1) % count) for i in range(count)])  8.48 us
    all_to_all x1, blocking collectives, local(): lax.all_to_all(arranged, 'lat', split_axis=1, concat_axis=1, tiled=True)  8.3 us
    all_to_all x1, blocking collectives, local(): lax.all_to_all(height, 'lon', split_axis=1, concat_axis=2, tiled=True)  7.73 us
    all_to_all x1, blocking collectives, local(): lax.all_to_all(grid_rows, 'lon', split_axis=2, concat_axis=1, tiled=True)  7.41 us
  transfers between devices with their start and end apart: 43, of which 33 were waited for; matrix products, arithmetic and copies ran while one was open for 5% of the time, Pallas kernels for 0%

commit v1 on v0

--- a/solution.py
+++ b/solution.py
@@ -138,7 +138,10 @@
     ) - jnp.einsum(
         "mx,mfr->frx", sin_full * doubling[:, None], returned[:, 1], precision=exact_mode
     )
-    loading = lax.all_to_all(grid_rows, "lon", split_axis=2, concat_axis=1, tiled=True)
+    loading = jnp.concatenate(
+        lax.all_to_all(jnp.stack(jnp.split(grid_rows, lax.axis_size("lon"), axis=2)), "lon", 0, 0),
+        axis=1,
+    )
     height = height + wetness * loading
     return advance(height, east_flow, north_flow)
 

time: 255 us -> 266 us (1.043)
  waiting for transfers between devices: 106 us -> 123 us
  local copies, waits for them, and re-layouts: 29.8 us -> 24 us
    ppermute x20, waiting for transfers between devices: 53.3 us -> 63.8 us  [with_halo(): lax.ppermute(head, axis, [((i + 1) % count, i) for i in range(count)])]
    ppermute x20, waiting for transfers between devices: 41.6 us -> 48.2 us  [with_halo(): lax.ppermute(tail, axis, [(i, (i + 1) % count) for i in range(count)])]
    unnamed x13 -> x14, local copies, waits for them, and re-layouts: 4.86 us -> 0.65 us
where the time goes in v1:
time: 266 us; the launch traced here: 265 us
  waiting for transfers between devices  123 us (46%)
  starting transfers between devices  70 us (26%)
  local copies, waits for them, and re-layouts  24 us (9%)
  blocking collectives  23.8 us (9%)
  matrix products  16.7 us (6%)
  other arithmetic  6.66 us (3%)
    ppermute x20, waiting for transfers between devices, with_halo(): lax.ppermute(head, axis, [((i + 1) % count, i) for i in range(count)])  63.8 us
    ppermute x20, starting transfers between devices, with_halo(): lax.ppermute(head, axis, [((i + 1) % count, i) for i in range(count)])  52.5 us
    ppermute x20, waiting for transfers between devices, with_halo(): lax.ppermute(tail, axis, [(i, (i + 1) % count) for i in range(count)])  48.2 us
    gather x24, local copies, waits for them, and re-layouts  11 us
    all_to_all x1, blocking collectives, local(): lax.all_to_all(arranged, 'lat', split_axis=1, concat_axis=1, tiled=True)  8.3 us
    all_to_all x1, blocking collectives, local(): lax.all_to_all(height, 'lon', split_axis=1, concat_axis=2, tiled=True)  8.06 us
    all_to_all x1, blocking collectives, local(): lax.all_to_all(jnp.stack(jnp.split(grid_rows, lax.axis_size('lon'), axis=...  7.41 us
    dot_general x1, matrix products, spherical(): jnp.einsum('kcn,kirn->kicr', coefficients, legendre_blocks, preferred_ele...  7.06 us
  transfers between devices with their start and end apart: 43, of which 33 were waited for; matrix products, arithmetic and copies ran while one was open for 5% of the time, Pallas kernels for 0%

profile of v1, /device:TPU:0, one launch (start us, length us, event | category | flops | bytes accessed | tf_op | source)
XLA Modules:
  0.0 265.1 jit_solution(13085371641310010426)
XLA Ops:
  2.9 4.1 %collective-permute-start.1 = (f32[1,8,1,128]{3,2,1,0:T(1,128)S(1)}, f32[1,8,1,128]{3,2,1,0:T(1,128)S(1)}, u32[]{:S(2)}, u32[]{:S(2)}) collective-permute-start(f32[1,8,1,128]{3,2,1,0:T(1,128)S(1)} %get-tuple-element.69), channel_id=1, source_target_pairs={{4,0},{8,4},{12,8},{16,12},{20,16},{24,20},{28,24},{0,28},{5,1},{9... | collective-permute-start | bytes 12296 | tf_op jit(solution)/shard_map/ppermute | solution.py:21
  8.4 2.9 %collective-permute-start.2 = (f32[1,8,34,1]{3,2,1,0:T(8,128)S(1)}, f32[1,8,34,1]{3,2,1,0:T(8,128)S(1)}, u32[]{:S(2)}, u32[]{:S(2)}) collective-permute-start(f32[1,8,34,1]{3,2,1,0:T(8,128)S(1)} %get-tuple-element.55), channel_id=1, source_target_pairs={{1,0},{2,1},{3,2},{0,3},{5,4},{6,5},{7,6},{4,7},{9,8},{10,9},{11,1... | collective-permute-start | bytes 3272 | tf_op jit(solution)/shard_map/ppermute | solution.py:21
  12.1 3.9 %collective-permute-done.2 = f32[1,8,34,1]{3,2,1,0:T(8,128)S(1)} collective-permute-done((f32[1,8,34,1]{3,2,1,0:T(8,128)S(1)}, f32[1,8,34,1]{3,2,1,0:T(8,128)S(1)}, u32[]{:S(2)}, u32[]{:S(2)}) %collective-permute-start.2) | collective-permute-done | bytes 1120 | tf_op jit(solution)/shard_map/ppermute | solution.py:21
  16.0 3.6 %collective-permute-done.3 = f32[1,8,34,1]{3,2,1,0:T(8,128)S(1)} collective-permute-done((f32[1,8,34,1]{3,2,1,0:T(8,128)S(1)}, f32[1,8,34,1]{3,2,1,0:T(8,128)S(1)}, u32[]{:S(2)}, u32[]{:S(2)}) %collective-permute-start.3) | collective-permute-done | bytes 1120 | tf_op jit(solution)/shard_map/ppermute | solution.py:19
  20.8 3.5 %collective-permute-start.5 = (f32[2,8,1,128]{3,2,1,0:T(1,128)S(1)}, f32[2,8,1,128]{3,2,1,0:T(1,128)S(1)}, u32[]{:S(2)}, u32[]{:S(2)}) collective-permute-start(f32[2,8,1,128]{3,2,1,0:T(1,128)S(1)} %get-tuple-element.40), channel_id=1, source_target_pairs={{4,0},{8,4},{12,8},{16,12},{20,16},{24,20},{28,24},{0,28},{5,1},{9... | collective-permute-start | bytes 24584 | tf_op jit(solution)/shard_map/ppermute | solution.py:21
  28.0 8.6 %collective-permute-done.6 = f32[2,8,34,1]{3,2,1,0:T(8,128)S(1)} collective-permute-done((f32[2,8,34,1]{3,2,1,0:T(8,128)S(1)}, f32[2,8,34,1]{3,2,1,0:T(8,128)S(1)}, u32[]{:S(2)}, u32[]{:S(2)}) %collective-permute-start.6) | collective-permute-done | bytes 2208 | tf_op jit(solution)/shard_map/ppermute | solution.py:21
  36.6 4.3 %collective-permute-done.7 = f32[2,8,34,1]{3,2,1,0:T(8,128)S(1)} collective-permute-done((f32[2,8,34,1]{3,2,1,0:T(8,128)S(1)}, f32[2,8,34,1]{3,2,1,0:T(8,128)S(1)}, u32[]{:S(2)}, u32[]{:S(2)}) %collective-permute-start.7) | collective-permute-done | bytes 2208 | tf_op jit(solution)/shard_map/ppermute | solution.py:19
  41.1 3.5 %collective-permute-start.9 = (f32[1,8,1,128]{3,2,1,0:T(1,128)S(1)}, f32[1,8,1,128]{3,2,1,0:T(1,128)S(1)}, u32[]{:S(2)}, u32[]{:S(2)}) collective-permute-start(f32[1,8,1,128]{3,2,1,0:T(1,128)S(1)} %get-tuple-element.67), channel_id=1, source_target_pairs={{4,0},{8,4},{12,8},{16,12},{20,16},{24,20},{28,24},{0,28},{5,1},{9... | collective-permute-start | bytes 12296 | tf_op jit(solution)/shard_map/ppermute | solution.py:21
  46.1 2.5 collective-permute-start.10
  48.6 4.2 %collective-permute-done.10 = f32[1,8,34,1]{3,2,1,0:T(8,128)S(1)} collective-permute-done((f32[1,8,34,1]{3,2,1,0:T(8,128)S(1)}, f32[1,8,34,1]{3,2,1,0:T(8,128)S(1)}, u32[]{:S(2)}, u32[]{:S(2)}) %collective-permute-start.10) | collective-permute-done | bytes 1120 | tf_op jit(solution)/shard_map/ppermute | solution.py:21
  52.9 2.7 %collective-permute-done.11 = f32[1,8,34,1]{3,2,1,0:T(8,128)S(1)} collective-permute-done((f32[1,8,34,1]{3,2,1,0:T(8,128)S(1)}, f32[1,8,34,1]{3,2,1,0:T(8,128)S(1)}, u32[]{:S(2)}, u32[]{:S(2)}) %collective-permute-start.11) | collective-permute-done | bytes 1120 | tf_op jit(solution)/shard_map/ppermute | solution.py:19
  55.8 3.5 %collective-permute-start.13 = (f32[2,8,1,128]{3,2,1,0:T(1,128)S(1)}, f32[2,8,1,128]{3,2,1,0:T(1,128)S(1)}, u32[]{:S(2)}, u32[]{:S(2)}) collective-permute-start(f32[2,8,1,128]{3,2,1,0:T(1,128)S(1)} %get-tuple-element.38), channel_id=1, source_target_pairs={{4,0},{8,4},{12,8},{16,12},{20,16},{24,20},{28,24},{0,28},{5,1},{9... | collective-permute-start | bytes 24584 | tf_op jit(solution)/shard_map/ppermute | solution.py:21
  63.0 8.6 %collective-permute-done.14 = f32[2,8,34,1]{3,2,1,0:T(8,128)S(1)} collective-permute-done((f32[2,8,34,1]{3,2,1,0:T(8,128)S(1)}, f32[2,8,34,1]{3,2,1,0:T(8,128)S(1)}, u32[]{:S(2)}, u32[]{:S(2)}) %collective-permute-start.14) | collective-permute-done | bytes 2208 | tf_op jit(solution)/shard_map/ppermute | solution.py:21
  71.6 3.9 %collective-permute-done.15 = f32[2,8,34,1]{3,2,1,0:T(8,128)S(1)} collective-permute-done((f32[2,8,34,1]{3,2,1,0:T(8,128)S(1)}, f32[2,8,34,1]{3,2,1,0:T(8,128)S(1)}, u32[]{:S(2)}, u32[]{:S(2)}) %collective-permute-start.15) | collective-permute-done | bytes 2208 | tf_op jit(solution)/shard_map/ppermute | solution.py:19
  75.8 3.5 %collective-permute-start.17 = (f32[1,8,1,128]{3,2,1,0:T(1,128)S(1)}, f32[1,8,1,128]{3,2,1,0:T(1,128)S(1)}, u32[]{:S(2)}, u32[]{:S(2)}) collective-permute-start(f32[1,8,1,128]{3,2,1,0:T(1,128)S(1)} %get-tuple-element.65), channel_id=1, source_target_pairs={{4,0},{8,4},{12,8},{16,12},{20,16},{24,20},{28,24},{0,28},{5,1},{9... | collective-permute-start | bytes 12296 | tf_op jit(solution)/shard_map/ppermute | solution.py:21
  80.8 2.3 collective-permute-start.18
  83.1 3.5 %collective-permute-done.18 = f32[1,8,34,1]{3,2,1,0:T(8,128)S(1)} collective-permute-done((f32[1,8,34,1]{3,2,1,0:T(8,128)S(1)}, f32[1,8,34,1]{3,2,1,0:T(8,128)S(1)}, u32[]{:S(2)}, u32[]{:S(2)}) %collective-permute-start.18) | collective-permute-done | bytes 1120 | tf_op jit(solution)/shard_map/ppermute | solution.py:21
  86.7 2.6 collective-permute-done.19
  89.5 3.5 %collective-permute-start.21 = (f32[2,8,1,128]{3,2,1,0:T(1,128)S(1)}, f32[2,8,1,128]{3,2,1,0:T(1,128)S(1)}, u32[]{:S(2)}, u32[]{:S(2)}) collective-permute-start(f32[2,8,1,128]{3,2,1,0:T(1,128)S(1)} %get-tuple-element.36), channel_id=1, source_target_pairs={{4,0},{8,4},{12,8},{16,12},{20,16},{24,20},{28,24},{0,28},{5,1},{9... | collective-permute-start | bytes 24584 | tf_op jit(solution)/shard_map/ppermute | solution.py:21
  96.7 8.6 %collective-permute-done.22 = f32[2,8,34,1]{3,2,1,0:T(8,128)S(1)} collective-permute-done((f32[2,8,34,1]{3,2,1,0:T(8,128)S(1)}, f32[2,8,34,1]{3,2,1,0:T(8,128)S(1)}, u32[]{:S(2)}, u32[]{:S(2)}) %collective-permute-start.22) | collective-permute-done | bytes 2208 | tf_op jit(solution)/shard_map/ppermute | solution.py:21
  105.3 3.9 %collective-permute-done.23 = f32[2,8,34,1]{3,2,1,0:T(8,128)S(1)} collective-permute-done((f32[2,8,34,1]{3,2,1,0:T(8,128)S(1)}, f32[2,8,34,1]{3,2,1,0:T(8,128)S(1)}, u32[]{:S(2)}, u32[]{:S(2)}) %collective-permute-start.23) | collective-permute-done | bytes 2208 | tf_op jit(solution)/shard_map/ppermute | solution.py:19
  109.5 3.5 %collective-permute-start.25 = (f32[1,8,1,128]{3,2,1,0:T(1,128)S(1)}, f32[1,8,1,128]{3,2,1,0:T(1,128)S(1)}, u32[]{:S(2)}, u32[]{:S(2)}) collective-permute-start(f32[1,8,1,128]{3,2,1,0:T(1,128)S(1)} %get-tuple-element.63), channel_id=1, source_target_pairs={{4,0},{8,4},{12,8},{16,12},{20,16},{24,20},{28,24},{0,28},{5,1},{9... | collective-permute-start | bytes 12296 | tf_op jit(solution)/shard_map/ppermute | solution.py:21
  114.5 1.9 collective-permute-start.26
  116.6 4.1 %collective-permute-done.26 = f32[1,8,34,1]{3,2,1,0:T(8,128)S(1)} collective-permute-done((f32[1,8,34,1]{3,2,1,0:T(8,128)S(1)}, f32[1,8,34,1]{3,2,1,0:T(8,128)S(1)}, u32[]{:S(2)}, u32[]{:S(2)}) %collective-permute-start.26) | collective-permute-done | bytes 1120 | tf_op jit(solution)/shard_map/ppermute | solution.py:21
  120.6 2.7 %collective-permute-done.27 = f32[1,8,34,1]{3,2,1,0:T(8,128)S(1)} collective-permute-done((f32[1,8,34,1]{3,2,1,0:T(8,128)S(1)}, f32[1,8,34,1]{3,2,1,0:T(8,128)S(1)}, u32[]{:S(2)}, u32[]{:S(2)}) %collective-permute-start.27) | collective-permute-done | bytes 1120 | tf_op jit(solution)/shard_map/ppermute | solution.py:19
  123.6 3.5 %collective-permute-start.29 = (f32[2,8,1,128]{3,2,1,0:T(1,128)S(1)}, f32[2,8,1,128]{3,2,1,0:T(1,128)S(1)}, u32[]{:S(2)}, u32[]{:S(2)}) collective-permute-start(f32[2,8,1,128]{3,2,1,0:T(1,128)S(1)} %get-tuple-element.34), channel_id=1, source_target_pairs={{4,0},{8,4},{12,8},{16,12},{20,16},{24,20},{28,24},{0,28},{5,1},{9... | collective-permute-start | bytes 24584 | tf_op jit(solution)/shard_map/ppermute | solution.py:21
  130.9 8.6 %collective-permute-done.30 = f32[2,8,34,1]{3,2,1,0:T(8,128)S(1)} collective-permute-done((f32[2,8,34,1]{3,2,1,0:T(8,128)S(1)}, f32[2,8,34,1]{3,2,1,0:T(8,128)S(1)}, u32[]{:S(2)}, u32[]{:S(2)}) %collective-permute-start.30) | collective-permute-done | bytes 2208 | tf_op jit(solution)/shard_map/ppermute | solution.py:21
  139.4 4.3 %collective-permute-done.31 = f32[2,8,34,1]{3,2,1,0:T(8,128)S(1)} collective-permute-done((f32[2,8,34,1]{3,2,1,0:T(8,128)S(1)}, f32[2,8,34,1]{3,2,1,0:T(8,128)S(1)}, u32[]{:S(2)}, u32[]{:S(2)}) %collective-permute-start.31) | collective-permute-done | bytes 2208 | tf_op jit(solution)/shard_map/ppermute | solution.py:19
  144.0 8.1 %all_to_all.43 = f32[8,32,128]{2,0,1:T(8,128)S(1)} all-to-all(f32[8,32,128]{2,0,1:T(8,128)S(1)} %copy.29), channel_id=1, replica_groups=mesh['lat'=8,'lon'=4] {'lon'}, dimensions={1} | all-to-all | bytes 262144 | tf_op jit(solution)/shard_map/all_to_all | solution.py:108
  152.1 2.5 fusion.5
  154.6 2.5 fusion.6
  160.2 3.4 %all-to-all-start.1 = ((bf16[4,8,1024]{2,0,1:T(4,128)(2,1)}), bf16[4,8,1024]{2,0,1:T(4,128)(2,1)S(1)}, u32[]{:S(2)}, u32[]{:S(2)}) async-start(bf16[4,8,1024]{2,0,1:T(4,128)(2,1)} %copy.32), calls=%async_computation.1 | async-start | bytes 131072 | tf_op jit(solution)/shard_map/all_to_all | solution.py:114
  163.6 5.8 %all-to-all-done.1 = bf16[4,8,1024]{2,0,1:T(4,128)(2,1)S(1)} async-done(((bf16[4,8,1024]{2,0,1:T(4,128)(2,1)}), bf16[4,8,1024]{2,0,1:T(4,128)(2,1)S(1)}, u32[]{:S(2)}, u32[]{:S(2)}) %all-to-all-start.1) | async-done | bytes 65568 | tf_op jit(solution)/shard_map/all_to_all | solution.py:114
  170.1 3.5 %all-to-all-start.2 = ((bf16[4,8,1024]{2,1,0:T(8,128)(2,1)}), bf16[4,8,1024]{2,1,0:T(8,128)(2,1)S(1)}, u32[]{:S(2)}, u32[]{:S(2)}) async-start(bf16[4,8,1024]{2,1,0:T(8,128)(2,1)} %copy.33), calls=%async_computation.2 | async-start | bytes 131072 | tf_op jit(solution)/shard_map/all_to_all | solution.py:113
  173.7 11.2 %while.1 = (s32[]{:T(128)}, f32[1280]{0:T(1024)S(1)}, s32[8,1]{0,1:T(1,128)S(1)}, f32[8,1024]{1,0:T(8,128)S(1)}, s32[]{:T(128)}, /*index=5*/s32[]{:T(128)}) while((s32[]{:T(128)}, f32[1280]{0:T(1024)S(1)}, s32[8,1]{0,1:T(1,128)S(1)}, f32[8,1024]{1,0:T(8,128)S(1)}, s32[]{:T(128)}, /*index=5*/s32[]{:T(128)}) %tuple.47), condition=%wide.while_cond, body=%wide.while_body.sunk | while | flops 2 | bytes 16473 | solution.py:104
  188.0 7.1 %fusion.3 = bf16[8,8,16,32]{3,2,1,0:T(8,128)(2,1)S(1)} fusion(bf16[8,8,32,1024]{3,2,1,0:T(8,128)(2,1)} %bitcast.223, bf16[8,8,16,32]{3,2,1,0:T(8,128)(2,1)S(1)} %reshape_reshape.3, f32[8,1024]{1,0:T(8,128)S(1)} %get-tuple-element.10), kind=kOutput, calls=%fused_computation.6 | convolution fusion | flops 134512640 | bytes 4358144 | tf_op jit(solution)/shard_map/kcn,kirn->kicr/dot_general | solution.py:63
  197.2 8.3 %all_to_all.44 = bf16[4,8,1024]{2,0,1:T(4,128)(2,1)S(1)} all-to-all(bf16[4,8,1024]{2,0,1:T(4,128)(2,1)S(1)} %copy.36), channel_id=1, replica_groups=mesh['lat'=8,'lon'=4] {'lat'}, dimensions={1} | all-to-all | bytes 131072 | tf_op jit(solution)/shard_map/all_to_all | solution.py:128
  206.2 3.9 %all-to-all-start.4 = ((bf16[4,8,1024]{2,1,0:T(8,128)(2,1)}), bf16[4,8,1024]{2,1,0:T(8,128)(2,1)S(1)}, u32[]{:S(2)}, u32[]{:S(2)}) async-start(bf16[4,8,1024]{2,1,0:T(8,128)(2,1)} %copy.37), calls=%async_computation.4 | async-start | bytes 131072 | tf_op jit(solution)/shard_map/all_to_all | solution.py:127
  210.1 4.8 %all-to-all-done.4 = bf16[4,8,1024]{2,1,0:T(8,128)(2,1)S(1)} async-done(((bf16[4,8,1024]{2,1,0:T(8,128)(2,1)}), bf16[4,8,1024]{2,1,0:T(8,128)(2,1)S(1)}, u32[]{:S(2)}, u32[]{:S(2)}) %all-to-all-start.4) | async-done | bytes 65568 | tf_op jit(solution)/shard_map/all_to_all | solution.py:127
  216.9 2.3 fusion.11
  219.2 2.3 convolution_subtract_fusion
  221.5 7.4 %all_to_all.45 = f32[4,8,8,128]{3,2,1,0:T(8,128)S(1)} all-to-all(f32[4,8,8,128]{3,2,1,0:T(8,128)S(1)} %pad_maximum_fusion.110), channel_id=1, replica_groups=mesh['lat'=8,'lon'=4] {'lon'}, dimensions={0} | all-to-all | bytes 262144 | tf_op jit(solution)/shard_map/all_to_all | solution.py:142
  229.0 3.5 %collective-permute-start.33 = (f32[1,8,1,128]{3,2,1,0:T(1,128)S(1)}, f32[1,8,1,128]{3,2,1,0:T(1,128)S(1)}, u32[]{:S(2)}, u32[]{:S(2)}) collective-permute-start(f32[1,8,1,128]{3,2,1,0:T(1,128)S(1)} %get-tuple-element.57), channel_id=1, source_target_pairs={{4,0},{8,4},{12,8},{16,12},{20,16},{24,20},{28,24},{0,28},{5,1},{9... | collective-permute-start | bytes 12296 | tf_op jit(solution)/shard_map/ppermute | solution.py:21
  236.2 4.9 %collective-permute-done.34 = f32[1,8,34,1]{3,2,1,0:T(8,128)S(1)} collective-permute-done((f32[1,8,34,1]{3,2,1,0:T(8,128)S(1)}, f32[1,8,34,1]{3,2,1,0:T(8,128)S(1)}, u32[]{:S(2)}, u32[]{:S(2)}) %collective-permute-start.34) | collective-permute-done | bytes 1120 | tf_op jit(solution)/shard_map/ppermute | solution.py:21
  241.2 2.2 collective-permute-done.35
  243.7 3.5 %collective-permute-start.37 = (f32[2,8,1,128]{3,2,1,0:T(1,128)S(1)}, f32[2,8,1,128]{3,2,1,0:T(1,128)S(1)}, u32[]{:S(2)}, u32[]{:S(2)}) collective-permute-start(f32[2,8,1,128]{3,2,1,0:T(1,128)S(1)} %get-tuple-element.32), channel_id=1, source_target_pairs={{4,0},{8,4},{12,8},{16,12},{20,16},{24,20},{28,24},{0,28},{5,1},{9... | collective-permute-start | bytes 24584 | tf_op jit(solution)/shard_map/ppermute | solution.py:21
  250.8 8.6 %collective-permute-done.38 = f32[2,8,34,1]{3,2,1,0:T(8,128)S(1)} collective-permute-done((f32[2,8,34,1]{3,2,1,0:T(8,128)S(1)}, f32[2,8,34,1]{3,2,1,0:T(8,128)S(1)}, u32[]{:S(2)}, u32[]{:S(2)}) %collective-permute-start.38) | collective-permute-done | bytes 2208 | tf_op jit(solution)/shard_map/ppermute | solution.py:21
  259.4 4.9 %collective-permute-done.39 = f32[2,8,34,1]{3,2,1,0:T(8,128)S(1)} collective-permute-done((f32[2,8,34,1]{3,2,1,0:T(8,128)S(1)}, f32[2,8,34,1]{3,2,1,0:T(8,128)S(1)}, u32[]{:S(2)}, u32[]{:S(2)}) %collective-permute-start.39) | collective-permute-done | bytes 2208 | tf_op jit(solution)/shard_map/ppermute | solution.py:19
  (154 shorter events, 57.8 us)
Async XLA Ops:
  0.6 40.2 %copy-start.2 = (f32[8,32,128]{2,1,0:T(8,128)S(1)}, f32[8,32,128]{2,1,0:T(8,128)}, u32[]{:S(2)}) copy-start(f32[8,32,128]{2,1,0:T(8,128)} %param.9) | copy-start | bytes 393220
  0.6 27.4 %copy-start.3 = (f32[32,128]{1,0:T(8,128)S(1)}, f32[32,128]{1,0:T(8,128)}, u32[]{:S(2)}) copy-start(f32[32,128]{1,0:T(8,128)} %param.12) | copy-start | bytes 49156
  2.3 5.9 %collective-permute-start = (f32[1,8,1,128]{3,2,1,0:T(1,128)S(1)}, f32[1,8,1,128]{3,2,1,0:T(1,128)S(1)}, u32[]{:S(2)}, u32[]{:S(2)}) collective-permute-start(f32[1,8,1,128]{3,2,1,0:T(1,128)S(1)} %get-tuple-element.70), channel_id=1, source_target_pairs={{0,4},{4,8},{8,12},{12,16},{16,20},{20,24},{24,28},{28,0},{1,5},{5... | collective-permute-start | bytes 12296 | tf_op jit(solution)/shard_map/ppermute | solution.py:19
  2.9 5.4 %collective-permute-start.1 = (f32[1,8,1,128]{3,2,1,0:T(1,128)S(1)}, f32[1,8,1,128]{3,2,1,0:T(1,128)S(1)}, u32[]{:S(2)}, u32[]{:S(2)}) collective-permute-start(f32[1,8,1,128]{3,2,1,0:T(1,128)S(1)} %get-tuple-element.69), channel_id=1, source_target_pairs={{4,0},{8,4},{12,8},{16,12},{20,16},{24,20},{28,24},{0,28},{5,1},{9... | collective-permute-start | bytes 12296 | tf_op jit(solution)/shard_map/ppermute | solution.py:21
  8.4 7.5 %collective-permute-start.2 = (f32[1,8,34,1]{3,2,1,0:T(8,128)S(1)}, f32[1,8,34,1]{3,2,1,0:T(8,128)S(1)}, u32[]{:S(2)}, u32[]{:S(2)}) collective-permute-start(f32[1,8,34,1]{3,2,1,0:T(8,128)S(1)} %get-tuple-element.55), channel_id=1, source_target_pairs={{1,0},{2,1},{3,2},{0,3},{5,4},{6,5},{7,6},{4,7},{9,8},{10,9},{11,1... | collective-permute-start | bytes 3272 | tf_op jit(solution)/shard_map/ppermute | solution.py:21
  11.4 8.2 %collective-permute-start.3 = (f32[1,8,34,1]{3,2,1,0:T(8,128)S(1)}, f32[1,8,34,1]{3,2,1,0:T(8,128)S(1)}, u32[]{:S(2)}, u32[]{:S(2)}) collective-permute-start(f32[1,8,34,1]{3,2,1,0:T(8,128)S(1)} %get-tuple-element.56), channel_id=1, source_target_pairs={{0,1},{1,2},{2,3},{3,0},{4,5},{5,6},{6,7},{7,4},{8,9},{9,10},{10,1... | collective-permute-start | bytes 3272 | tf_op jit(solution)/shard_map/ppermute | solution.py:19
  20.8 4.9 %collective-permute-start.4 = (f32[2,8,1,128]{3,2,1,0:T(1,128)S(1)}, f32[2,8,1,128]{3,2,1,0:T(1,128)S(1)}, u32[]{:S(2)}, u32[]{:S(2)}) collective-permute-start(f32[2,8,1,128]{3,2,1,0:T(1,128)S(1)} %get-tuple-element.39), channel_id=1, source_target_pairs={{0,4},{4,8},{8,12},{12,16},{16,20},{20,24},{24,28},{28,0},{1,5},{5... | collective-permute-start | bytes 24584 | tf_op jit(solution)/shard_map/ppermute | solution.py:19
  20.8 4.9 %collective-permute-start.5 = (f32[2,8,1,128]{3,2,1,0:T(1,128)S(1)}, f32[2,8,1,128]{3,2,1,0:T(1,128)S(1)}, u32[]{:S(2)}, u32[]{:S(2)}) collective-permute-start(f32[2,8,1,128]{3,2,1,0:T(1,128)S(1)} %get-tuple-element.40), channel_id=1, source_target_pairs={{4,0},{8,4},{12,8},{16,12},{20,16},{24,20},{28,24},{0,28},{5,1},{9... | collective-permute-start | bytes 24584 | tf_op jit(solution)/shard_map/ppermute | solution.py:21
  25.9 10.6 %collective-permute-start.6 = (f32[2,8,34,1]{3,2,1,0:T(8,128)S(1)}, f32[2,8,34,1]{3,2,1,0:T(8,128)S(1)}, u32[]{:S(2)}, u32[]{:S(2)}) collective-permute-start(f32[2,8,34,1]{3,2,1,0:T(8,128)S(1)} %get-tuple-element.30), channel_id=1, source_target_pairs={{1,0},{2,1},{3,2},{0,3},{5,4},{6,5},{7,6},{4,7},{9,8},{10,9},{11,1... | collective-permute-start | bytes 6536 | tf_op jit(solution)/shard_map/ppermute | solution.py:21
  27.4 13.4 %collective-permute-start.7 = (f32[2,8,34,1]{3,2,1,0:T(8,128)S(1)}, f32[2,8,34,1]{3,2,1,0:T(8,128)S(1)}, u32[]{:S(2)}, u32[]{:S(2)}) collective-permute-start(f32[2,8,34,1]{3,2,1,0:T(8,128)S(1)} %get-tuple-element.29), channel_id=1, source_target_pairs={{0,1},{1,2},{2,3},{3,0},{4,5},{5,6},{6,7},{7,4},{8,9},{9,10},{10,1... | collective-permute-start | bytes 6536 | tf_op jit(solution)/shard_map/ppermute | solution.py:19
  41.1 4.9 %collective-permute-start.8 = (f32[1,8,1,128]{3,2,1,0:T(1,128)S(1)}, f32[1,8,1,128]{3,2,1,0:T(1,128)S(1)}, u32[]{:S(2)}, u32[]{:S(2)}) collective-permute-start(f32[1,8,1,128]{3,2,1,0:T(1,128)S(1)} %get-tuple-element.68), channel_id=1, source_target_pairs={{0,4},{4,8},{8,12},{12,16},{16,20},{20,24},{24,28},{28,0},{1,5},{5... | collective-permute-start | bytes 12296 | tf_op jit(solution)/shard_map/ppermute | solution.py:19
  41.1 4.9 %collective-permute-start.9 = (f32[1,8,1,128]{3,2,1,0:T(1,128)S(1)}, f32[1,8,1,128]{3,2,1,0:T(1,128)S(1)}, u32[]{:S(2)}, u32[]{:S(2)}) collective-permute-start(f32[1,8,1,128]{3,2,1,0:T(1,128)S(1)} %get-tuple-element.67), channel_id=1, source_target_pairs={{4,0},{8,4},{12,8},{16,12},{20,16},{24,20},{28,24},{0,28},{5,1},{9... | collective-permute-start | bytes 12296 | tf_op jit(solution)/shard_map/ppermute | solution.py:21
  46.1 6.7 %collective-permute-start.10 = (f32[1,8,34,1]{3,2,1,0:T(8,128)S(1)}, f32[1,8,34,1]{3,2,1,0:T(8,128)S(1)}, u32[]{:S(2)}, u32[]{:S(2)}) collective-permute-start(f32[1,8,34,1]{3,2,1,0:T(8,128)S(1)} %get-tuple-element.53), channel_id=1, source_target_pairs={{1,0},{2,1},{3,2},{0,3},{5,4},{6,5},{7,6},{4,7},{9,8},{10,9},{11,1... | collective-permute-start | bytes 3272 | tf_op jit(solution)/shard_map/ppermute | solution.py:21
  48.6 6.9 %collective-permute-start.11 = (f32[1,8,34,1]{3,2,1,0:T(8,128)S(1)}, f32[1,8,34,1]{3,2,1,0:T(8,128)S(1)}, u32[]{:S(2)}, u32[]{:S(2)}) collective-permute-start(f32[1,8,34,1]{3,2,1,0:T(8,128)S(1)} %get-tuple-element.54), channel_id=1, source_target_pairs={{0,1},{1,2},{2,3},{3,0},{4,5},{5,6},{6,7},{7,4},{8,9},{9,10},{10,1... | collective-permute-start | bytes 3272 | tf_op jit(solution)/shard_map/ppermute | solution.py:19
  55.8 4.9 %collective-permute-start.12 = (f32[2,8,1,128]{3,2,1,0:T(1,128)S(1)}, f32[2,8,1,128]{3,2,1,0:T(1,128)S(1)}, u32[]{:S(2)}, u32[]{:S(2)}) collective-permute-start(f32[2,8,1,128]{3,2,1,0:T(1,128)S(1)} %get-tuple-element.37), channel_id=1, source_target_pairs={{0,4},{4,8},{8,12},{12,16},{16,20},{20,24},{24,28},{28,0},{1,5},{5... | collective-permute-start | bytes 24584 | tf_op jit(solution)/shard_map/ppermute | solution.py:19
  55.8 4.9 %collective-permute-start.13 = (f32[2,8,1,128]{3,2,1,0:T(1,128)S(1)}, f32[2,8,1,128]{3,2,1,0:T(1,128)S(1)}, u32[]{:S(2)}, u32[]{:S(2)}) collective-permute-start(f32[2,8,1,128]{3,2,1,0:T(1,128)S(1)} %get-tuple-element.38), channel_id=1, source_target_pairs={{4,0},{8,4},{12,8},{16,12},{20,16},{24,20},{28,24},{0,28},{5,1},{9... | collective-permute-start | bytes 24584 | tf_op jit(solution)/shard_map/ppermute | solution.py:21
  60.9 10.6 %collective-permute-start.14 = (f32[2,8,34,1]{3,2,1,0:T(8,128)S(1)}, f32[2,8,34,1]{3,2,1,0:T(8,128)S(1)}, u32[]{:S(2)}, u32[]{:S(2)}) collective-permute-start(f32[2,8,34,1]{3,2,1,0:T(8,128)S(1)} %get-tuple-element.28), channel_id=1, source_target_pairs={{1,0},{2,1},{3,2},{0,3},{5,4},{6,5},{7,6},{4,7},{9,8},{10,9},{11,1... | collective-permute-start | bytes 6536 | tf_op jit(solution)/shard_map/ppermute | solution.py:21
  62.1 13.4 %collective-permute-start.15 = (f32[2,8,34,1]{3,2,1,0:T(8,128)S(1)}, f32[2,8,34,1]{3,2,1,0:T(8,128)S(1)}, u32[]{:S(2)}, u32[]{:S(2)}) collective-permute-start(f32[2,8,34,1]{3,2,1,0:T(8,128)S(1)} %get-tuple-element.27), channel_id=1, source_target_pairs={{0,1},{1,2},{2,3},{3,0},{4,5},{5,6},{6,7},{7,4},{8,9},{9,10},{10,1... | collective-permute-start | bytes 6536 | tf_op jit(solution)/shard_map/ppermute | solution.py:19
  75.7 4.9 %collective-permute-start.16 = (f32[1,8,1,128]{3,2,1,0:T(1,128)S(1)}, f32[1,8,1,128]{3,2,1,0:T(1,128)S(1)}, u32[]{:S(2)}, u32[]{:S(2)}) collective-permute-start(f32[1,8,1,128]{3,2,1,0:T(1,128)S(1)} %get-tuple-element.66), channel_id=1, source_target_pairs={{0,4},{4,8},{8,12},{12,16},{16,20},{20,24},{24,28},{28,0},{1,5},{5... | collective-permute-start | bytes 12296 | tf_op jit(solution)/shard_map/ppermute | solution.py:19
  75.8 4.9 %collective-permute-start.17 = (f32[1,8,1,128]{3,2,1,0:T(1,128)S(1)}, f32[1,8,1,128]{3,2,1,0:T(1,128)S(1)}, u32[]{:S(2)}, u32[]{:S(2)}) collective-permute-start(f32[1,8,1,128]{3,2,1,0:T(1,128)S(1)} %get-tuple-element.65), channel_id=1, source_target_pairs={{4,0},{8,4},{12,8},{16,12},{20,16},{24,20},{28,24},{0,28},{5,1},{9... | collective-permute-start | bytes 12296 | tf_op jit(solution)/shard_map/ppermute | solution.py:21
  80.8 5.9 %collective-permute-start.18 = (f32[1,8,34,1]{3,2,1,0:T(8,128)S(1)}, f32[1,8,34,1]{3,2,1,0:T(8,128)S(1)}, u32[]{:S(2)}, u32[]{:S(2)}) collective-permute-start(f32[1,8,34,1]{3,2,1,0:T(8,128)S(1)} %get-tuple-element.51), channel_id=1, source_target_pairs={{1,0},{2,1},{3,2},{0,3},{5,4},{6,5},{7,6},{4,7},{9,8},{10,9},{11,1... | collective-permute-start | bytes 3272 | tf_op jit(solution)/shard_map/ppermute | solution.py:21
  83.0 6.2 %collective-permute-start.19 = (f32[1,8,34,1]{3,2,1,0:T(8,128)S(1)}, f32[1,8,34,1]{3,2,1,0:T(8,128)S(1)}, u32[]{:S(2)}, u32[]{:S(2)}) collective-permute-start(f32[1,8,34,1]{3,2,1,0:T(8,128)S(1)} %get-tuple-element.52), channel_id=1, source_target_pairs={{0,1},{1,2},{2,3},{3,0},{4,5},{5,6},{6,7},{7,4},{8,9},{9,10},{10,1... | collective-permute-start | bytes 3272 | tf_op jit(solution)/shard_map/ppermute | solution.py:19
  89.5 4.9 %collective-permute-start.20 = (f32[2,8,1,128]{3,2,1,0:T(1,128)S(1)}, f32[2,8,1,128]{3,2,1,0:T(1,128)S(1)}, u32[]{:S(2)}, u32[]{:S(2)}) collective-permute-start(f32[2,8,1,128]{3,2,1,0:T(1,128)S(1)} %get-tuple-element.35), channel_id=1, source_target_pairs={{0,4},{4,8},{8,12},{12,16},{16,20},{20,24},{24,28},{28,0},{1,5},{5... | collective-permute-start | bytes 24584 | tf_op jit(solution)/shard_map/ppermute | solution.py:19
  89.5 4.9 %collective-permute-start.21 = (f32[2,8,1,128]{3,2,1,0:T(1,128)S(1)}, f32[2,8,1,128]{3,2,1,0:T(1,128)S(1)}, u32[]{:S(2)}, u32[]{:S(2)}) collective-permute-start(f32[2,8,1,128]{3,2,1,0:T(1,128)S(1)} %get-tuple-element.36), channel_id=1, source_target_pairs={{4,0},{8,4},{12,8},{16,12},{20,16},{24,20},{28,24},{0,28},{5,1},{9... | collective-permute-start | bytes 24584 | tf_op jit(solution)/shard_map/ppermute | solution.py:21
  94.5 57.6 %copy-start.5 = (s32[256]{0:T(256)S(1)}, s32[256]{0:T(256)}, u32[]{:S(2)}) copy-start(s32[256]{0:T(256)} %param.17) | copy-start | bytes 3076
  94.7 10.6 %collective-permute-start.22 = (f32[2,8,34,1]{3,2,1,0:T(8,128)S(1)}, f32[2,8,34,1]{3,2,1,0:T(8,128)S(1)}, u32[]{:S(2)}, u32[]{:S(2)}) collective-permute-start(f32[2,8,34,1]{3,2,1,0:T(8,128)S(1)} %get-tuple-element.26), channel_id=1, source_target_pairs={{1,0},{2,1},{3,2},{0,3},{5,4},{6,5},{7,6},{4,7},{9,8},{10,9},{11,1... | collective-permute-start | bytes 6536 | tf_op jit(solution)/shard_map/ppermute | solution.py:21
  95.7 13.5 %collective-permute-start.23 = (f32[2,8,34,1]{3,2,1,0:T(8,128)S(1)}, f32[2,8,34,1]{3,2,1,0:T(8,128)S(1)}, u32[]{:S(2)}, u32[]{:S(2)}) collective-permute-start(f32[2,8,34,1]{3,2,1,0:T(8,128)S(1)} %get-tuple-element.25), channel_id=1, source_target_pairs={{0,1},{1,2},{2,3},{3,0},{4,5},{5,6},{6,7},{7,4},{8,9},{9,10},{10,1... | collective-permute-start | bytes 6536 | tf_op jit(solution)/shard_map/ppermute | solution.py:19
  109.4 4.9 %collective-permute-start.24 = (f32[1,8,1,128]{3,2,1,0:T(1,128)S(1)}, f32[1,8,1,128]{3,2,1,0:T(1,128)S(1)}, u32[]{:S(2)}, u32[]{:S(2)}) collective-permute-start(f32[1,8,1,128]{3,2,1,0:T(1,128)S(1)} %get-tuple-element.64), channel_id=1, source_target_pairs={{0,4},{4,8},{8,12},{12,16},{16,20},{20,24},{24,28},{28,0},{1,5},{5... | collective-permute-start | bytes 12296 | tf_op jit(solution)/shard_map/ppermute | solution.py:19
  109.5 4.9 %collective-permute-start.25 = (f32[1,8,1,128]{3,2,1,0:T(1,128)S(1)}, f32[1,8,1,128]{3,2,1,0:T(1,128)S(1)}, u32[]{:S(2)}, u32[]{:S(2)}) collective-permute-start(f32[1,8,1,128]{3,2,1,0:T(1,128)S(1)} %get-tuple-element.63), channel_id=1, source_target_pairs={{4,0},{8,4},{12,8},{16,12},{20,16},{24,20},{28,24},{0,28},{5,1},{9... | collective-permute-start | bytes 12296 | tf_op jit(solution)/shard_map/ppermute | solution.py:21
  114.5 6.2 %collective-permute-start.26 = (f32[1,8,34,1]{3,2,1,0:T(8,128)S(1)}, f32[1,8,34,1]{3,2,1,0:T(8,128)S(1)}, u32[]{:S(2)}, u32[]{:S(2)}) collective-permute-start(f32[1,8,34,1]{3,2,1,0:T(8,128)S(1)} %get-tuple-element.49), channel_id=1, source_target_pairs={{1,0},{2,1},{3,2},{0,3},{5,4},{6,5},{7,6},{4,7},{9,8},{10,9},{11,1... | collective-permute-start | bytes 3272 | tf_op jit(solution)/shard_map/ppermute | solution.py:21
  116.4 6.9 %collective-permute-start.27 = (f32[1,8,34,1]{3,2,1,0:T(8,128)S(1)}, f32[1,8,34,1]{3,2,1,0:T(8,128)S(1)}, u32[]{:S(2)}, u32[]{:S(2)}) collective-permute-start(f32[1,8,34,1]{3,2,1,0:T(8,128)S(1)} %get-tuple-element.50), channel_id=1, source_target_pairs={{0,1},{1,2},{2,3},{3,0},{4,5},{5,6},{6,7},{7,4},{8,9},{9,10},{10,1... | collective-permute-start | bytes 3272 | tf_op jit(solution)/shard_map/ppermute | solution.py:19
  123.6 5.0 %collective-permute-start.28 = (f32[2,8,1,128]{3,2,1,0:T(1,128)S(1)}, f32[2,8,1,128]{3,2,1,0:T(1,128)S(1)}, u32[]{:S(2)}, u32[]{:S(2)}) collective-permute-start(f32[2,8,1,128]{3,2,1,0:T(1,128)S(1)} %get-tuple-element.33), channel_id=1, source_target_pairs={{0,4},{4,8},{8,12},{12,16},{16,20},{20,24},{24,28},{28,0},{1,5},{5... | collective-permute-start | bytes 24584 | tf_op jit(solution)/shard_map/ppermute | solution.py:19
  123.6 4.9 %collective-permute-start.29 = (f32[2,8,1,128]{3,2,1,0:T(1,128)S(1)}, f32[2,8,1,128]{3,2,1,0:T(1,128)S(1)}, u32[]{:S(2)}, u32[]{:S(2)}) collective-permute-start(f32[2,8,1,128]{3,2,1,0:T(1,128)S(1)} %get-tuple-element.34), channel_id=1, source_target_pairs={{4,0},{8,4},{12,8},{16,12},{20,16},{24,20},{28,24},{0,28},{5,1},{9... | collective-permute-start | bytes 24584 | tf_op jit(solution)/shard_map/ppermute | solution.py:21
  128.8 10.6 %collective-permute-start.30 = (f32[2,8,34,1]{3,2,1,0:T(8,128)S(1)}, f32[2,8,34,1]{3,2,1,0:T(8,128)S(1)}, u32[]{:S(2)}, u32[]{:S(2)}) collective-permute-start(f32[2,8,34,1]{3,2,1,0:T(8,128)S(1)} %get-tuple-element.24), channel_id=1, source_target_pairs={{1,0},{2,1},{3,2},{0,3},{5,4},{6,5},{7,6},{4,7},{9,8},{10,9},{11,1... | collective-permute-start | bytes 6536 | tf_op jit(solution)/shard_map/ppermute | solution.py:21
  129.8 13.9 %collective-permute-start.31 = (f32[2,8,34,1]{3,2,1,0:T(8,128)S(1)}, f32[2,8,34,1]{3,2,1,0:T(8,128)S(1)}, u32[]{:S(2)}, u32[]{:S(2)}) collective-permute-start(f32[2,8,34,1]{3,2,1,0:T(8,128)S(1)} %get-tuple-element.23), channel_id=1, source_target_pairs={{0,1},{1,2},{2,3},{3,0},{4,5},{5,6},{6,7},{7,4},{8,9},{9,10},{10,1... | collective-permute-start | bytes 6536 | tf_op jit(solution)/shard_map/ppermute | solution.py:19
  143.9 29.8 %copy-start.4 = (f32[256]{0:T(256)S(1)}, f32[256]{0:T(256)}, u32[]{:S(2)}) copy-start(f32[256]{0:T(256)} %param.16) | copy-start | bytes 3076
  160.2 9.2 %all-to-all-start.1 = ((bf16[4,8,1024]{2,0,1:T(4,128)(2,1)}), bf16[4,8,1024]{2,0,1:T(4,128)(2,1)S(1)}, u32[]{:S(2)}, u32[]{:S(2)}) async-start(bf16[4,8,1024]{2,0,1:T(4,128)(2,1)} %copy.32), calls=%async_computation.1 | async-start | bytes 131072 | tf_op jit(solution)/shard_map/all_to_all | solution.py:114
  170.1 14.8 %all-to-all-start.2 = ((bf16[4,8,1024]{2,1,0:T(8,128)(2,1)}), bf16[4,8,1024]{2,1,0:T(8,128)(2,1)S(1)}, u32[]{:S(2)}, u32[]{:S(2)}) async-start(bf16[4,8,1024]{2,1,0:T(8,128)(2,1)} %copy.33), calls=%async_computation.2 | async-start | bytes 131072 | tf_op jit(solution)/shard_map/all_to_all | solution.py:113
  206.2 8.8 %all-to-all-start.4 = ((bf16[4,8,1024]{2,1,0:T(8,128)(2,1)}), bf16[4,8,1024]{2,1,0:T(8,128)(2,1)S(1)}, u32[]{:S(2)}, u32[]{:S(2)}) async-start(bf16[4,8,1024]{2,1,0:T(8,128)(2,1)} %copy.37), calls=%async_computation.4 | async-start | bytes 131072 | tf_op jit(solution)/shard_map/all_to_all | solution.py:127
  229.0 4.9 %collective-permute-start.32 = (f32[1,8,1,128]{3,2,1,0:T(1,128)S(1)}, f32[1,8,1,128]{3,2,1,0:T(1,128)S(1)}, u32[]{:S(2)}, u32[]{:S(2)}) collective-permute-start(f32[1,8,1,128]{3,2,1,0:T(1,128)S(1)} %get-tuple-element.58), channel_id=1, source_target_pairs={{0,4},{4,8},{8,12},{12,16},{16,20},{20,24},{24,28},{28,0},{1,5},{5... | collective-permute-start | bytes 12296 | tf_op jit(solution)/shard_map/ppermute | solution.py:19
  229.0 4.9 %collective-permute-start.33 = (f32[1,8,1,128]{3,2,1,0:T(1,128)S(1)}, f32[1,8,1,128]{3,2,1,0:T(1,128)S(1)}, u32[]{:S(2)}, u32[]{:S(2)}) collective-permute-start(f32[1,8,1,128]{3,2,1,0:T(1,128)S(1)} %get-tuple-element.57), channel_id=1, source_target_pairs={{4,0},{8,4},{12,8},{16,12},{20,16},{24,20},{28,24},{0,28},{5,1},{9... | collective-permute-start | bytes 12296 | tf_op jit(solution)/shard_map/ppermute | solution.py:21
  234.0 7.1 %collective-permute-start.34 = (f32[1,8,34,1]{3,2,1,0:T(8,128)S(1)}, f32[1,8,34,1]{3,2,1,0:T(8,128)S(1)}, u32[]{:S(2)}, u32[]{:S(2)}) collective-permute-start(f32[1,8,34,1]{3,2,1,0:T(8,128)S(1)} %get-tuple-element.47), channel_id=1, source_target_pairs={{1,0},{2,1},{3,2},{0,3},{5,4},{6,5},{7,6},{4,7},{9,8},{10,9},{11,1... | collective-permute-start | bytes 3272 | tf_op jit(solution)/shard_map/ppermute | solution.py:21
  234.8 8.6 %collective-permute-start.35 = (f32[1,8,34,1]{3,2,1,0:T(8,128)S(1)}, f32[1,8,34,1]{3,2,1,0:T(8,128)S(1)}, u32[]{:S(2)}, u32[]{:S(2)}) collective-permute-start(f32[1,8,34,1]{3,2,1,0:T(8,128)S(1)} %get-tuple-element.48), channel_id=1, source_target_pairs={{0,1},{1,2},{2,3},{3,0},{4,5},{5,6},{6,7},{7,4},{8,9},{9,10},{10,1... | collective-permute-start | bytes 3272 | tf_op jit(solution)/shard_map/ppermute | solution.py:19
  236.2 28.9 %copy-start = (f32[8,32,128]{2,1,0:T(8,128)}, f32[8,32,128]{2,1,0:T(8,128)S(1)}, u32[]{:S(2)}) copy-start(f32[8,32,128]{2,1,0:T(8,128)S(1)} %fusion.40) | copy-start | bytes 393220
  243.6 4.9 %collective-permute-start.36 = (f32[2,8,1,128]{3,2,1,0:T(1,128)S(1)}, f32[2,8,1,128]{3,2,1,0:T(1,128)S(1)}, u32[]{:S(2)}, u32[]{:S(2)}) collective-permute-start(f32[2,8,1,128]{3,2,1,0:T(1,128)S(1)} %get-tuple-element.31), channel_id=1, source_target_pairs={{0,4},{4,8},{8,12},{12,16},{16,20},{20,24},{24,28},{28,0},{1,5},{5... | collective-permute-start | bytes 24584 | tf_op jit(solution)/shard_map/ppermute | solution.py:19
  243.7 4.9 %collective-permute-start.37 = (f32[2,8,1,128]{3,2,1,0:T(1,128)S(1)}, f32[2,8,1,128]{3,2,1,0:T(1,128)S(1)}, u32[]{:S(2)}, u32[]{:S(2)}) collective-permute-start(f32[2,8,1,128]{3,2,1,0:T(1,128)S(1)} %get-tuple-element.32), channel_id=1, source_target_pairs={{4,0},{8,4},{12,8},{16,12},{20,16},{24,20},{28,24},{0,28},{5,1},{9... | collective-permute-start | bytes 24584 | tf_op jit(solution)/shard_map/ppermute | solution.py:21
  248.8 10.6 %collective-permute-start.38 = (f32[2,8,34,1]{3,2,1,0:T(8,128)S(1)}, f32[2,8,34,1]{3,2,1,0:T(8,128)S(1)}, u32[]{:S(2)}, u32[]{:S(2)}) collective-permute-start(f32[2,8,34,1]{3,2,1,0:T(8,128)S(1)} %get-tuple-element.22), channel_id=1, source_target_pairs={{1,0},{2,1},{3,2},{0,3},{5,4},{6,5},{7,6},{4,7},{9,8},{10,9},{11,1... | collective-permute-start | bytes 6536 | tf_op jit(solution)/shard_map/ppermute | solution.py:21
  250.3 14.0 %collective-permute-start.39 = (f32[2,8,34,1]{3,2,1,0:T(8,128)S(1)}, f32[2,8,34,1]{3,2,1,0:T(8,128)S(1)}, u32[]{:S(2)}, u32[]{:S(2)}) collective-permute-start(f32[2,8,34,1]{3,2,1,0:T(8,128)S(1)} %get-tuple-element.21), channel_id=1, source_target_pairs={{0,1},{1,2},{2,3},{3,0},{4,5},{5,6},{6,7},{7,4},{8,9},{9,10},{10,1... | collective-permute-start | bytes 6536 | tf_op jit(solution)/shard_map/ppermute | solution.py:19
  (1 other events, 21.6 us)
